TPU v7x, 32 devices: a whole 2x2x4 slice. The times are simulated.
32 devices in a mesh: view: 2 (over y), tile: 16 (over z, x, core).
Axes of the slice: x: 2, y: 2, z: 4, core: 2. Of those that a mesh axis runs over, the one named last changes fastest.
Arguments:
- estimate: float32 [8, 512, 512], P(None, 'tile'), may hold values from 0.5 to 2
- observed: float32 [2, 8, 512, 512], P('view', None, 'tile'), may hold values from 0.2 to 4
- psf_taps: float32 [2, 3, 31], P('view'), may hold values from 0.05 to 1
Outputs:
- restored: float32 [8, 512, 512], P(None, 'tile')
All inputs are finite; a program needn't handle non-finite values.
Results may differ from a plain program's by a relative error of at most 0.0001.
Values sent between devices are 32-bit elements; how exact they have to be, the bound alone decides.
No kernel may reach another device: no remote copies, remote signals or barrier semaphores. Data moves between devices by JAX's collectives and lax.ppermute only.
A program may use at most 64 MiB of HBM per device.

v0:
```python
import jax
import jax.numpy as jnp
from jax import lax
from jax.sharding import PartitionSpec as P

ITERS = 2


def extended_2(cells, sides, width):
    for axis, dim in sides:
        count = lax.axis_size(axis)
        ends = count - 1
        head = lax.slice_in_dim(cells, 0, width, axis=dim)
        tail = lax.slice_in_dim(cells, cells.shape[dim] - width, cells.shape[dim], axis=dim)
        cells = jnp.concatenate(
            [
                lax.ppermute(tail, axis, [(i, (i + 1) % count) for i in range(ends)]),
                cells,
                lax.ppermute(head, axis, [((i + 1) % count, i) for i in range(ends)]),
            ],
            axis=dim,
        )
    return cells


def band_matrix(taps, count_in, count_out, offset):
    rows_in = jnp.arange(count_in)[:, None]
    cols_out = jnp.arange(count_out)[None, :]
    lag = rows_in - cols_out + offset
    length = taps.shape[0]
    inside = (lag >= 0) & (lag < length)
    return jnp.where(inside, jnp.take(taps, jnp.clip(lag, 0, length - 1)), 0.0)


def many_bands(taps, count_in, count_out, offset):
    return jax.vmap(lambda one: band_matrix(one, count_in, count_out, offset))(taps)


def blur(field, z_mats, y_mats, x_taps, cols_out):
    highest = lax.Precision.HIGHEST
    if field.ndim == 3:
        out = jnp.einsum("kyx,vkz->vzyx", field, z_mats, precision=highest)
    else:
        out = jnp.einsum("vkyx,vkz->vzyx", field, z_mats, precision=highest)
    out = jnp.einsum("vzjx,vjy->vzyx", out, y_mats, precision=highest)
    reach = (x_taps.shape[1] - 1) // 2
    pieces = []
    for start in range(0, cols_out, 128):
        block = min(128, cols_out - start)
        x_mats = many_bands(x_taps, block + 2 * reach, block, 0)
        piece = lax.slice_in_dim(out, start, start + block + 2 * reach, axis=3)
        pieces.append(jnp.einsum("vzyj,vjx->vzyx", piece, x_mats, precision=highest))
    return jnp.concatenate(pieces, axis=3)


def body(estimate, observed, psf_taps):
    depth, rows, width = estimate.shape
    half = (psf_taps.shape[2] - 1) // 2
    views = lax.axis_size("view")
    recorded = lax.all_to_all(observed, "view", split_axis=3, concat_axis=0, tiled=True)
    taps = lax.all_gather(psf_taps, "view", axis=0, tiled=True)
    cols = width // views
    col_start = lax.axis_index("view") * cols
    current = lax.dynamic_slice_in_dim(estimate, col_start, cols, 2)
    normed = taps / jnp.sum(taps, axis=2, keepdims=True)
    flipped = normed[:, :, ::-1]
    fwd_z = many_bands(normed[:, 0], depth, depth, half)
    back_z = many_bands(flipped[:, 0], depth, depth, half)
    back_y = many_bands(flipped[:, 1], rows + 2 * half, rows, 0)
    fwd_y = many_bands(normed[:, 1], rows + 2 * half, rows, 0)
    for step in range(ITERS):
        extended = extended_2(current, (("view", 2), ("tile", 1)), half)
        blurred = blur(extended, fwd_z, fwd_y, normed[:, 2], cols)
        ratio = recorded / blurred
        ratio_ext = extended_2(ratio, (("view", 3), ("tile", 2)), half)
        log_corr = jnp.log(blur(ratio_ext, back_z, back_y, flipped[:, 2], cols))
        log_total = jnp.sum(log_corr, axis=0)
        current = current * jnp.exp(log_total / views)
    current = lax.all_gather(current, "view", axis=2, tiled=True)
    return current


def solution(mesh):
    placed = (P(None, "tile", None), P("view", None, "tile", None), P("view", None, None))
    return jax.shard_map(
        body, mesh=mesh, in_specs=placed, out_specs=P(None, "tile", None), check_vma=False
    )
```

profile of v0, /device:TPU:9, one launch (start us, length us, event | category | flops | bytes accessed | tf_op | source)
XLA Modules:
  0.0 232.1 jit_solution(4656722165472639557)
XLA Ops:
  2.0 3.8 %collective-permute-start = (f32[8,32,15]{2,0,1:T(8,128)}, f32[8,32,15]{2,0,1:T(8,128)}, u32[]{:S(2)}, u32[]{:S(2)}) collective-permute-start(f32[8,32,15]{2,0,1:T(8,128)} %get-tuple-element.22), channel_id=1, source_target_pairs={{0,16},{1,17},{2,18},{3,19},{4,20},{5,21},{6,22},{7,23},{8,24},{9,... | collective-permute-start | bytes 46088 | tf_op jit(solution)/shard_map/ppermute | solution.py:17
  9.5 4.0 %all-to-all-start = ((f32[2,1,65536]{2,1,0:T(1,128)}), f32[2,1,65536]{2,1,0:T(1,128)S(1)}, u32[]{:S(2)}, u32[]{:S(2)}) async-start(f32[2,1,65536]{2,1,0:T(1,128)} %reshape.110), calls=%async_computation | async-start | bytes 1048576 | tf_op jit(solution)/shard_map/all_to_all | solution.py:60
  13.6 7.8 %all_gather.6 = f32[2,3,31]{2,1,0:T(4,128)S(1)} all-gather(f32[1,3,31]{2,1,0:T(4,128)S(1)} %copy.97), channel_id=1, replica_groups=mesh['view'=2,'tile'=16] {'view'}, dimensions={0}, use_global_device_ids=true | all-gather | bytes 1116 | tf_op jit(solution)/shard_map/all_gather | solution.py:61
  23.1 4.9 %collective-permute-start.2 = (f32[8,15,286]{2,0,1:T(8,128)S(1)}, f32[8,15,286]{2,0,1:T(8,128)S(1)}, u32[]{:S(2)}, u32[]{:S(2)}) collective-permute-start(f32[8,15,286]{2,0,1:T(8,128)S(1)} %get-tuple-element.18), channel_id=1, source_target_pairs={{0,1},{1,2},{2,3},{3,4},{4,5},{5,6},{6,7},{7,8},{8,9},{9,10},{10,1... | collective-permute-start | bytes 411848 | tf_op jit(solution)/shard_map/ppermute | solution.py:17
  30.9 5.6 %gather_fusion.2 = f32[1984,2]{1,0:T(8,128)S(1)} fusion(f32[2,31]{0,1:T(8,128)S(1)} %copy.107, s32[2048]{0:T(1024)S(1)} %pad_clamp_fusion.1), kind=kCustom, calls=%fused_computation.3.clone | custom fusion | bytes 39680 | tf_op jit(solution)/shard_map/vmap(jit(_take))/gather | solution.py:32
  37.2 37.8 %gather_fusion.4 = f32[20224,2]{1,0:T(8,128)} fusion(f32[2,31]{0,1:T(8,128)S(1)} %copy.113, s32[20480]{0:T(1024)S(1)} %pad_clamp_fusion), kind=kCustom, calls=%fused_computation.2.clone | custom fusion | bytes 404480 | tf_op jit(solution)/shard_map/vmap(jit(_take))/gather | solution.py:32
  75.0 6.0 %copy.114 = f32[158,128,2]{1,0,2:T(8,128)S(1)} copy(f32[158,128,2]{2,1,0:T(8,128)} %bitcast.150) | data formatting | bytes 323584 | tf_op jit(solution)/shard_map/vmap(jit(_take))/gather | solution.py:32
  81.0 2.5 %fusion.24 = f32[2,8,62,286]{3,1,2,0:T(8,128)S(1)} fusion(f32[8,15,286]{2,0,1:T(8,128)} %collective-permute-done.3, f32[8,32,15]{2,0,1:T(8,128)} %collective-permute-done.1, f32[8,32,256]{2,0,1:T(8,128)S(1)} %copy.148, f32[8,32,15]{2,0,1:T(8,128)} %collective-permute-done, f32[8,15,286]{2,0,1:T(8,128)S(1)} %collective-permute-done.2, ...), kind=kOutput, calls=%fused_computation.27 | convolution fusion | flops 27804032 | bytes 1702912 | tf_op jit(solution)/shard_map/kyx,vkz->vzyx/dot_general | solution.py:42
  87.8 2.3 reduce
  95.6 2.8 %collective-permute-done.4 = f32[2,8,32,15]{3,2,1,0:T(8,128)S(1)} collective-permute-done((f32[2,8,32,15]{3,2,1,0:T(8,128)S(1)}, f32[2,8,32,15]{3,2,1,0:T(8,128)S(1)}, u32[]{:S(2)}, u32[]{:S(2)}) %collective-permute-start.4) | collective-permute-done | bytes 30752 | tf_op jit(solution)/shard_map/ppermute | solution.py:17
  98.4 3.8 %collective-permute-done.5 = f32[2,8,32,15]{3,2,1,0:T(8,128)S(1)} collective-permute-done((f32[2,8,32,15]{3,2,1,0:T(8,128)S(1)}, f32[2,8,32,15]{3,2,1,0:T(8,128)S(1)}, u32[]{:S(2)}, u32[]{:S(2)}) %collective-permute-start.5) | collective-permute-done | bytes 30752 | tf_op jit(solution)/shard_map/ppermute | solution.py:19
  103.5 5.7 %collective-permute-start.6 = (f32[2,8,15,286]{3,2,1,0:T(8,128)}, f32[2,8,15,286]{3,2,1,0:T(8,128)}, u32[]{:S(2)}, u32[]{:S(2)}) collective-permute-start(f32[2,8,15,286]{3,2,1,0:T(8,128)} %get-tuple-element.10), channel_id=1, source_target_pairs={{0,1},{1,2},{2,3},{3,4},{4,5},{5,6},{6,7},{7,8},{8,9},{9,10},{10,1... | collective-permute-start | bytes 823688 | tf_op jit(solution)/shard_map/ppermute | solution.py:17
  112.7 5.6 %gather_fusion = f32[1984,2]{1,0:T(8,128)S(1)} fusion(f32[2,31]{0,1:T(8,128)S(1)} %copy.99, s32[2048]{0:T(1024)S(1)} %pad_clamp_fusion.1), kind=kCustom, calls=%fused_computation.clone | custom fusion | bytes 39680 | tf_op jit(solution)/shard_map/vmap(jit(_take))/gather | solution.py:32
  118.9 37.8 %gather_fusion.5 = f32[20224,2]{1,0:T(8,128)} fusion(f32[2,31]{0,1:T(8,128)S(1)} %copy.118, s32[20480]{0:T(1024)S(1)} %pad_clamp_fusion), kind=kCustom, calls=%fused_computation.5.clone | custom fusion | bytes 404480 | tf_op jit(solution)/shard_map/vmap(jit(_take))/gather | solution.py:32
  156.7 6.0 %copy.119 = f32[158,128,2]{1,0,2:T(8,128)S(1)} copy(f32[158,128,2]{2,1,0:T(8,128)} %bitcast.149) | data formatting | bytes 323584 | tf_op jit(solution)/shard_map/vmap(jit(_take))/gather | solution.py:32
  172.5 3.8 %collective-permute-done.9 = f32[8,32,15]{2,0,1:T(8,128)S(1)} collective-permute-done((f32[8,32,15]{2,0,1:T(8,128)S(1)}, f32[8,32,15]{2,0,1:T(8,128)S(1)}, u32[]{:S(2)}, u32[]{:S(2)}) %collective-permute-start.9) | collective-permute-done | bytes 15392 | tf_op jit(solution)/shard_map/ppermute | solution.py:19
  176.5 5.1 %collective-permute-start.10 = (f32[8,15,286]{2,0,1:T(8,128)S(1)}, f32[8,15,286]{2,0,1:T(8,128)S(1)}, u32[]{:S(2)}, u32[]{:S(2)}) collective-permute-start(f32[8,15,286]{2,0,1:T(8,128)S(1)} %get-tuple-element.14), channel_id=1, source_target_pairs={{0,1},{1,2},{2,3},{3,4},{4,5},{5,6},{6,7},{7,8},{8,9},{9,10},{10,1... | collective-permute-start | bytes 411848 | tf_op jit(solution)/shard_map/ppermute | solution.py:17
  184.1 4.4 %collective-permute-done.11 = f32[8,15,286]{2,0,1:T(8,128)S(1)} collective-permute-done((f32[8,15,286]{2,0,1:T(8,128)S(1)}, f32[8,15,286]{2,0,1:T(8,128)S(1)}, u32[]{:S(2)}, u32[]{:S(2)}) %collective-permute-start.11) | collective-permute-done | bytes 137312 | tf_op jit(solution)/shard_map/ppermute | solution.py:19
  195.1 4.1 %collective-permute-done.12 = f32[2,8,32,15]{3,2,1,0:T(8,128)S(1)} collective-permute-done((f32[2,8,32,15]{3,2,1,0:T(8,128)S(1)}, f32[2,8,32,15]{3,2,1,0:T(8,128)S(1)}, u32[]{:S(2)}, u32[]{:S(2)}) %collective-permute-start.12) | collective-permute-done | bytes 30752 | tf_op jit(solution)/shard_map/ppermute | solution.py:17
  199.2 3.8 %collective-permute-done.13 = f32[2,8,32,15]{3,2,1,0:T(8,128)S(1)} collective-permute-done((f32[2,8,32,15]{3,2,1,0:T(8,128)S(1)}, f32[2,8,32,15]{3,2,1,0:T(8,128)S(1)}, u32[]{:S(2)}, u32[]{:S(2)}) %collective-permute-start.13) | collective-permute-done | bytes 30752 | tf_op jit(solution)/shard_map/ppermute | solution.py:19
  205.4 3.5 %collective-permute-start.15 = (f32[2,8,15,286]{3,2,1,0:T(8,128)S(1)}, f32[2,8,15,286]{3,2,1,0:T(8,128)S(1)}, u32[]{:S(2)}, u32[]{:S(2)}) collective-permute-start(f32[2,8,15,286]{3,2,1,0:T(8,128)S(1)} %get-tuple-element.8), channel_id=1, source_target_pairs={{1,0},{2,1},{3,2},{4,3},{5,4},{6,5},{7,6},{8,7},{9,8},{10,9},{11,1... | collective-permute-start | bytes 823688 | tf_op jit(solution)/shard_map/ppermute | solution.py:19
  210.1 8.3 %collective-permute-done.15 = f32[2,8,15,286]{3,2,1,0:T(8,128)S(1)} collective-permute-done((f32[2,8,15,286]{3,2,1,0:T(8,128)S(1)}, f32[2,8,15,286]{3,2,1,0:T(8,128)S(1)}, u32[]{:S(2)}, u32[]{:S(2)}) %collective-permute-start.15) | collective-permute-done | bytes 274592 | tf_op jit(solution)/shard_map/ppermute | solution.py:19
  218.9 2.1 fusion.8
  223.6 7.4 %all_gather.7 = f32[8,32,512]{2,0,1:T(8,128)S(1)} all-gather(f32[8,32,256]{2,0,1:T(8,128)S(1)} %fusion.61), channel_id=1, replica_groups=mesh['view'=2,'tile'=16] {'view'}, dimensions={2}, use_global_device_ids=true | all-gather | bytes 786432 | tf_op jit(solution)/shard_map/all_gather | solution.py:79
  (102 shorter events, 52.8 us)
Async XLA Ops:
  0.0 1.0 copy-start
  0.0 7.1 %copy-start.3 = (f32[1,8,32,512]{3,2,1,0:T(8,128)S(1)}, f32[1,8,32,512]{3,2,1,0:T(8,128)}, u32[]{:S(2)}) copy-start(f32[1,8,32,512]{3,2,1,0:T(8,128)} %param.10) | copy-start | bytes 1572868
  1.1 4.7 %copy-start.1 = (f32[8,32,256]{2,1,0:T(8,128)}, f32[8,32,256]{2,1,0:T(8,128)S(1)}, u32[]{:S(2)}) copy-start(f32[8,32,256]{2,1,0:T(8,128)S(1)} %constant_dynamic-slice_fusion) | copy-start | bytes 786436
  2.0 19.9 %collective-permute-start = (f32[8,32,15]{2,0,1:T(8,128)}, f32[8,32,15]{2,0,1:T(8,128)}, u32[]{:S(2)}, u32[]{:S(2)}) collective-permute-start(f32[8,32,15]{2,0,1:T(8,128)} %get-tuple-element.22), channel_id=1, source_target_pairs={{0,16},{1,17},{2,18},{3,19},{4,20},{5,21},{6,22},{7,23},{8,24},{9,... | collective-permute-start | bytes 46088 | tf_op jit(solution)/shard_map/ppermute | solution.py:17
  5.8 16.1 %collective-permute-start.1 = (f32[8,32,15]{2,0,1:T(8,128)}, f32[8,32,15]{2,0,1:T(8,128)}, u32[]{:S(2)}, u32[]{:S(2)}) collective-permute-start(f32[8,32,15]{2,0,1:T(8,128)} %get-tuple-element.23), channel_id=1, source_target_pairs={{16,0},{17,1},{18,2},{19,3},{20,4},{21,5},{22,6},{23,7},{24,8},{25... | collective-permute-start | bytes 46088 | tf_op jit(solution)/shard_map/ppermute | solution.py:19
  7.9 5.7 %copy-start.4 = (f32[1,3,31]{2,0,1:T(1,128)S(1)}, f32[1,3,31]{2,0,1:T(1,128)}, u32[]{:S(2)}) copy-start(f32[1,3,31]{2,0,1:T(1,128)} %param.11) | copy-start | bytes 1120
  9.5 77.8 %all-to-all-start = ((f32[2,1,65536]{2,1,0:T(1,128)}), f32[2,1,65536]{2,1,0:T(1,128)S(1)}, u32[]{:S(2)}, u32[]{:S(2)}) async-start(f32[2,1,65536]{2,1,0:T(1,128)} %reshape.110), calls=%async_computation | async-start | bytes 1048576 | tf_op jit(solution)/shard_map/all_to_all | solution.py:60
  23.1 58.0 %collective-permute-start.2 = (f32[8,15,286]{2,0,1:T(8,128)S(1)}, f32[8,15,286]{2,0,1:T(8,128)S(1)}, u32[]{:S(2)}, u32[]{:S(2)}) collective-permute-start(f32[8,15,286]{2,0,1:T(8,128)S(1)} %get-tuple-element.18), channel_id=1, source_target_pairs={{0,1},{1,2},{2,3},{3,4},{4,5},{5,6},{6,7},{7,8},{8,9},{9,10},{10,1... | collective-permute-start | bytes 411848 | tf_op jit(solution)/shard_map/ppermute | solution.py:17
  28.0 53.1 %collective-permute-start.3 = (f32[8,15,286]{2,0,1:T(8,128)S(1)}, f32[8,15,286]{2,0,1:T(8,128)}, u32[]{:S(2)}, u32[]{:S(2)}) collective-permute-start(f32[8,15,286]{2,0,1:T(8,128)S(1)} %get-tuple-element.19), channel_id=1, source_target_pairs={{1,0},{2,1},{3,2},{4,3},{5,4},{6,5},{7,6},{8,7},{9,8},{10,9},{11,1... | collective-permute-start | bytes 411848 | tf_op jit(solution)/shard_map/ppermute | solution.py:19
  92.9 5.5 %collective-permute-start.4 = (f32[2,8,32,15]{3,2,1,0:T(8,128)S(1)}, f32[2,8,32,15]{3,2,1,0:T(8,128)S(1)}, u32[]{:S(2)}, u32[]{:S(2)}) collective-permute-start(f32[2,8,32,15]{3,2,1,0:T(8,128)S(1)} %get-tuple-element.16), channel_id=1, source_target_pairs={{0,16},{1,17},{2,18},{3,19},{4,20},{5,21},{6,22},{7,23},{8,24},{9,... | collective-permute-start | bytes 92168 | tf_op jit(solution)/shard_map/ppermute | solution.py:17
  94.3 7.9 %collective-permute-start.5 = (f32[2,8,32,15]{3,2,1,0:T(8,128)S(1)}, f32[2,8,32,15]{3,2,1,0:T(8,128)S(1)}, u32[]{:S(2)}, u32[]{:S(2)}) collective-permute-start(f32[2,8,32,15]{3,2,1,0:T(8,128)S(1)} %get-tuple-element.17), channel_id=1, source_target_pairs={{16,0},{17,1},{18,2},{19,3},{20,4},{21,5},{22,6},{23,7},{24,8},{25... | collective-permute-start | bytes 92168 | tf_op jit(solution)/shard_map/ppermute | solution.py:19
  103.5 59.2 %collective-permute-start.6 = (f32[2,8,15,286]{3,2,1,0:T(8,128)}, f32[2,8,15,286]{3,2,1,0:T(8,128)}, u32[]{:S(2)}, u32[]{:S(2)}) collective-permute-start(f32[2,8,15,286]{3,2,1,0:T(8,128)} %get-tuple-element.10), channel_id=1, source_target_pairs={{0,1},{1,2},{2,3},{3,4},{4,5},{5,6},{6,7},{7,8},{8,9},{9,10},{10,1... | collective-permute-start | bytes 823688 | tf_op jit(solution)/shard_map/ppermute | solution.py:17
  109.3 53.4 %collective-permute-start.7 = (f32[2,8,15,286]{3,2,1,0:T(8,128)}, f32[2,8,15,286]{3,2,1,0:T(8,128)}, u32[]{:S(2)}, u32[]{:S(2)}) collective-permute-start(f32[2,8,15,286]{3,2,1,0:T(8,128)} %get-tuple-element.11), channel_id=1, source_target_pairs={{1,0},{2,1},{3,2},{4,3},{5,4},{6,5},{7,6},{8,7},{9,8},{10,9},{11,1... | collective-permute-start | bytes 823688 | tf_op jit(solution)/shard_map/ppermute | solution.py:19
  167.5 1.3 copy-start.2
  169.3 3.2 %collective-permute-start.8 = (f32[8,32,15]{2,0,1:T(8,128)S(1)}, f32[8,32,15]{2,0,1:T(8,128)S(1)}, u32[]{:S(2)}, u32[]{:S(2)}) collective-permute-start(f32[8,32,15]{2,0,1:T(8,128)S(1)} %get-tuple-element.20), channel_id=1, source_target_pairs={{0,16},{1,17},{2,18},{3,19},{4,20},{5,21},{6,22},{7,23},{8,24},{9,... | collective-permute-start | bytes 46088 | tf_op jit(solution)/shard_map/ppermute | solution.py:17
  170.6 5.7 %collective-permute-start.9 = (f32[8,32,15]{2,0,1:T(8,128)S(1)}, f32[8,32,15]{2,0,1:T(8,128)S(1)}, u32[]{:S(2)}, u32[]{:S(2)}) collective-permute-start(f32[8,32,15]{2,0,1:T(8,128)S(1)} %get-tuple-element.21), channel_id=1, source_target_pairs={{16,0},{17,1},{18,2},{19,3},{20,4},{21,5},{22,6},{23,7},{24,8},{25... | collective-permute-start | bytes 46088 | tf_op jit(solution)/shard_map/ppermute | solution.py:19
  176.5 7.6 %collective-permute-start.10 = (f32[8,15,286]{2,0,1:T(8,128)S(1)}, f32[8,15,286]{2,0,1:T(8,128)S(1)}, u32[]{:S(2)}, u32[]{:S(2)}) collective-permute-start(f32[8,15,286]{2,0,1:T(8,128)S(1)} %get-tuple-element.14), channel_id=1, source_target_pairs={{0,1},{1,2},{2,3},{3,4},{4,5},{5,6},{6,7},{7,8},{8,9},{9,10},{10,1... | collective-permute-start | bytes 411848 | tf_op jit(solution)/shard_map/ppermute | solution.py:17
  181.6 6.9 %collective-permute-start.11 = (f32[8,15,286]{2,0,1:T(8,128)S(1)}, f32[8,15,286]{2,0,1:T(8,128)S(1)}, u32[]{:S(2)}, u32[]{:S(2)}) collective-permute-start(f32[8,15,286]{2,0,1:T(8,128)S(1)} %get-tuple-element.15), channel_id=1, source_target_pairs={{1,0},{2,1},{3,2},{4,3},{5,4},{6,5},{7,6},{8,7},{9,8},{10,9},{11,1... | collective-permute-start | bytes 411848 | tf_op jit(solution)/shard_map/ppermute | solution.py:19
  192.5 6.7 %collective-permute-start.12 = (f32[2,8,32,15]{3,2,1,0:T(8,128)S(1)}, f32[2,8,32,15]{3,2,1,0:T(8,128)S(1)}, u32[]{:S(2)}, u32[]{:S(2)}) collective-permute-start(f32[2,8,32,15]{3,2,1,0:T(8,128)S(1)} %get-tuple-element.12), channel_id=1, source_target_pairs={{0,16},{1,17},{2,18},{3,19},{4,20},{5,21},{6,22},{7,23},{8,24},{9,... | collective-permute-start | bytes 92168 | tf_op jit(solution)/shard_map/ppermute | solution.py:17
  193.8 9.2 %collective-permute-start.13 = (f32[2,8,32,15]{3,2,1,0:T(8,128)S(1)}, f32[2,8,32,15]{3,2,1,0:T(8,128)S(1)}, u32[]{:S(2)}, u32[]{:S(2)}) collective-permute-start(f32[2,8,32,15]{3,2,1,0:T(8,128)S(1)} %get-tuple-element.13), channel_id=1, source_target_pairs={{16,0},{17,1},{18,2},{19,3},{20,4},{21,5},{22,6},{23,7},{24,8},{25... | collective-permute-start | bytes 92168 | tf_op jit(solution)/shard_map/ppermute | solution.py:19
  203.5 6.6 %collective-permute-start.14 = (f32[2,8,15,286]{3,2,1,0:T(8,128)S(1)}, f32[2,8,15,286]{3,2,1,0:T(8,128)S(1)}, u32[]{:S(2)}, u32[]{:S(2)}) collective-permute-start(f32[2,8,15,286]{3,2,1,0:T(8,128)S(1)} %get-tuple-element.6), channel_id=1, source_target_pairs={{0,1},{1,2},{2,3},{3,4},{4,5},{5,6},{6,7},{7,8},{8,9},{9,10},{10,1... | collective-permute-start | bytes 823688 | tf_op jit(solution)/shard_map/ppermute | solution.py:17
  205.4 13.0 %collective-permute-start.15 = (f32[2,8,15,286]{3,2,1,0:T(8,128)S(1)}, f32[2,8,15,286]{3,2,1,0:T(8,128)S(1)}, u32[]{:S(2)}, u32[]{:S(2)}) collective-permute-start(f32[2,8,15,286]{3,2,1,0:T(8,128)S(1)} %get-tuple-element.8), channel_id=1, source_target_pairs={{1,0},{2,1},{3,2},{4,3},{5,4},{6,5},{7,6},{8,7},{9,8},{10,9},{11,1... | collective-permute-start | bytes 823688 | tf_op jit(solution)/shard_map/ppermute | solution.py:19
where the time goes:
time: 233 us; the launch traced here: 232 us
  local copies, waits for them, and re-layouts  111 us (48%)
  starting transfers between devices  44.1 us (19%)
  waiting for transfers between devices  33.4 us (14%)
  matrix products  18.9 us (8%)
  blocking collectives  15.2 us (7%)
  other arithmetic  8.52 us (4%)
    gather x12, local copies, waits for them, and re-layouts, band_matrix(): return jnp.where(inside, jnp.take(taps, jnp.clip(lag, 0, length - 1)), 0.0)  101 us
    ppermute x8, starting transfers between devices, extended_2(): lax.ppermute(tail, axis, [(i, (i + 1) % count) for i in range(ends)])  25.5 us
    ppermute x8, waiting for transfers between devices, extended_2(): lax.ppermute(head, axis, [((i + 1) % count, i) for i in range(ends)])  24.2 us
    ppermute x8, starting transfers between devices, extended_2(): lax.ppermute(head, axis, [((i + 1) % count, i) for i in range(ends)])  14.6 us
    ppermute x8, waiting for transfers between devices, extended_2(): lax.ppermute(tail, axis, [(i, (i + 1) % count) for i in range(ends)])  9.2 us
    all_gather x1, blocking collectives, body(): taps = lax.all_gather(psf_taps, 'view', axis=0, tiled=True)  7.85 us
    all_gather x1, blocking collectives, body(): current = lax.all_gather(current, 'view', axis=2, tiled=True)  7.4 us
    dot_general x8, matrix products, blur(): jnp.einsum('vzyj,vjx->vzyx', piece, x_mats, precision=highest)  6.3 us
  transfers between devices with their start and end apart: 17, of which 10 were waited for; matrix products, arithmetic and copies ran while one was open for 49% of the time, Pallas kernels for 0%

commit v1 on v0

--- a/solution.py
+++ b/solution.py
@@ -1,9 +1,421 @@
 import jax
 import jax.numpy as jnp
 from jax import lax
+from jax.experimental import pallas as pl
+from jax.experimental.pallas import tpu as pltpu
 from jax.sharding import PartitionSpec as P
 
 ITERS = 2
+LANES = 128
+BF = jnp.bfloat16
+F32 = jnp.float32
+VMEM = pl.BlockSpec(memory_space=pltpu.VMEM)
+SMEM = pl.BlockSpec(memory_space=pltpu.SMEM)
+
+
+def shaped(shape, dtype=F32):
+    return jax.ShapeDtypeStruct(shape, dtype)
+
+
+def split(cells):
+    high = cells.astype(BF)
+    return high, (cells - high.astype(F32)).astype(BF)
+
+
+def block_at(view, place, blocks):
+    at = jnp.where(view == 0, place, blocks - 1 - place)
+    return pl.ds(pl.multiple_of(at * LANES, LANES), LANES)
+
+
+def fold(planes, view, parts):
+    piece = LANES // parts
+    lane = lax.broadcasted_iota(jnp.int32, planes[0].shape, 1)
+    first = jnp.where(view == 0, 0, piece)
+    total = None
+    for at, plane in enumerate(planes):
+        moved = pltpu.roll(plane, lax.rem(first + at * piece, LANES), 1)
+        total = moved if total is None else jnp.where(lane >= at * piece, moved, total)
+    return total
+
+
+def unfold(folded, view, parts, at):
+    piece = LANES // parts
+    first = jnp.where(view == 0, LANES, LANES - piece)
+    return pltpu.roll(folded, lax.rem(first - at * piece, LANES), 1)
+
+
+def pack_window(view, planes_of, depth, own, parts, out_ref):
+    for place in range(own):
+        for z in range(depth):
+            out_ref[place * depth + z] = planes_of(z, place)
+    for group in range(depth // parts):
+        planes = [planes_of(group * parts + at, own) for at in range(parts)]
+        out_ref[own * depth + group] = fold(planes, view, parts)
+
+
+def unpack_window(view, packed_of, depth, own, parts, store):
+    for place in range(own):
+        for z in range(depth):
+            store(z, place, packed_of(place * depth + z))
+    for group in range(depth // parts):
+        folded = packed_of(own * depth + group)
+        for at in range(parts):
+            store(group * parts + at, own, unfold(folded, view, parts, at))
+
+
+def est_pack_kernel(meta, est, out):
+    depth, _, width = est.shape
+    own = width // LANES // 2
+    view = meta[0]
+    pack_window(
+        view, lambda z, p: est[z, :, block_at(view, p, width // LANES)], depth, own, 2, out
+    )
+
+
+def obs_pack_kernel(meta, obs, mine, theirs):
+    _, depth, _, width = obs.shape
+    own = width // LANES // 2
+    for view, out in ((meta[0], mine), (1 - meta[0], theirs)):
+        pack_window(
+            view,
+            lambda z, p, view=view: obs[0, z, :, block_at(view, p, width // LANES)],
+            depth,
+            own,
+            2,
+            out,
+        )
+
+
+def bands_kernel(meta, taps, y_out, x_out):
+    length = taps.shape[1]
+    reach = (length - 1) // 2
+    rows = y_out.shape[1]
+    span = 2 * rows
+    x_out[...] = jnp.zeros_like(x_out)
+    low = (LANES - reach) // 16 * 16
+    high = -(-(2 * LANES + reach) // 16) * 16
+    at_before = pl.multiple_of(jnp.where(meta[0] == 0, low, 2 * LANES + low), 16)
+    at_after = pl.multiple_of(jnp.where(meta[0] == 0, 2 * LANES, 0), 16)
+    in_at = lax.broadcasted_iota(jnp.int32, (high - low, LANES), 0) + low
+    out_at = lax.broadcasted_iota(jnp.int32, (high - low, LANES), 1)
+    lag = in_at - LANES - out_at
+    r_at = lax.broadcasted_iota(jnp.int32, (rows, 3 * span), 0)
+    s_at = lax.broadcasted_iota(jnp.int32, (rows, 3 * span), 1)
+    y_lag = lax.rem(s_at, span) - r_at - rows // 2
+    for back in range(2):
+        x_band = jnp.zeros(lag.shape, F32)
+        y_band = jnp.zeros(y_lag.shape, F32)
+        for tap in range(length):
+            at = tap - reach if back == 0 else reach - tap
+            x_band = jnp.where(lag == at, taps[2, tap], x_band)
+            y_band = jnp.where(y_lag == at, taps[1, tap], y_band)
+        x_high, x_low = split(x_band)
+        for which, cells in enumerate((x_high, x_low)):
+            before, after = LANES - low, high - 2 * LANES
+            x_out[back, which, pl.ds(at_before, before)] = cells[:before]
+            x_out[back, which, LANES : 2 * LANES] = cells[before : before + LANES]
+            x_out[back, which, pl.ds(at_after, after)] = cells[before + LANES :]
+        y_high = y_band.astype(BF).astype(F32)
+        y_out[back] = jnp.where(s_at < 2 * span, y_high, y_band - y_high).astype(BF)
+
+
+def spread_x(x_bands, back, own_mat, ext_mat):
+    own = own_mat.shape[1] // LANES
+    for part, which in enumerate((0, 1, 0)):
+        for src in range(own + 1):
+            at = (part * (own + 1) + src) * LANES
+            for dst in range(own):
+                if abs(src - dst) <= 1:
+                    start = (src - dst + 1) * LANES
+                    cells = x_bands[back, which, start : start + LANES, :]
+                else:
+                    cells = jnp.zeros((LANES, LANES), BF)
+                own_mat[at : at + LANES, dst * LANES : (dst + 1) * LANES] = cells
+        if ext_mat is not None:
+            for src in range(2):
+                at = (part * 2 + src) * LANES
+                ext_mat[at : at + LANES, :] = x_bands[back, which, src * LANES : (src + 1) * LANES, :]
+
+
+def y_stage(source, bands, lanes):
+    high, low = split(source)
+    return jnp.dot(bands, jnp.concatenate([high, low, high], axis=0), preferred_element_type=F32)
+
+
+def z_stage(taps, view, back, inner, base, rows, outer):
+    depth = inner.shape[0]
+    reach = (taps.shape[1] - 1) // 2
+    for row in range(0, rows, 8):
+        planes = [inner[z, base + row : base + row + 8, :] for z in range(depth)]
+        for out in range(depth):
+            total = None
+            for z in range(depth):
+                at = reach + (out - z if back else z - out)
+                term = taps[view, at] * planes[z]
+                total = term if total is None else total + term
+            outer[out, row : row + 8, :] = total
+
+
+def x_stage(cells, own_mat, ext_mat):
+    depth, rows, lanes = cells.shape
+    flat = cells.reshape(depth * rows, lanes)
+    high, low = split(flat)
+    left = jnp.concatenate([high, high, low], axis=1)
+    own = jnp.dot(left, own_mat[...], preferred_element_type=F32).reshape(depth, rows, -1)
+    if ext_mat is None:
+        return own, None
+    at = lanes - 2 * LANES
+    left = jnp.concatenate([high[:, at:], high[:, at:], low[:, at:]], axis=1)
+    ext = jnp.dot(left, ext_mat[...], preferred_element_type=F32).reshape(depth, rows, LANES)
+    return own, ext
+
+
+def forward(field, z_taps, y_bands, x_mats, inner, outer, emit):
+    depth = field.shape[0]
+    rows = outer.shape[1]
+    for half in range(2):
+        for z in range(depth):
+            inner[z] = y_stage(field[z, half * rows : half * rows + 2 * rows, :], y_bands, None)
+        for view in range(2):
+            z_stage(z_taps, view, False, inner, view * rows, rows, outer)
+            own, ext = x_stage(outer[...], *x_mats[view])
+            emit(view, half, own, ext)
+
+
+def backward(ratio, view, z_taps, y_band, x_mat, inner, outer):
+    depth = ratio.shape[0]
+    rows = outer.shape[1]
+    for z in range(depth):
+        inner[z, :rows, :] = y_stage(ratio[z], y_band, None)
+    z_stage(z_taps, view, True, inner, 0, rows, outer)
+    return x_stage(outer[...], *x_mat)
+
+
+def place_rows(even, rows):
+    at_a = pl.multiple_of(jnp.where(even == 1, 2 * rows, 0), rows)
+    at_b = pl.multiple_of(jnp.where(even == 1, 0, 2 * rows), rows)
+    return at_a, at_b
+
+
+def forward_kernel(meta, z_taps, est, got_a, got_b, y0, y1, x0, x1, blurred, field, inner, outer, *mats):
+    depth, rows, width = est.shape
+    own = width // LANES // 2
+    view = meta[0]
+    for place in range(own + 1):
+        lanes = slice(place * LANES, (place + 1) * LANES)
+        field[:, rows : 2 * rows, lanes] = est[:, :, block_at(view, place, width // LANES)]
+    for got, at in zip((got_a, got_b), place_rows(meta[1], rows)):
+
+        def store(z, place, cells, at=at):
+            field[z, pl.ds(at, rows), place * LANES : (place + 1) * LANES] = cells
+
+        unpack_window(view, lambda n, got=got: got[n], depth, own, 2, store)
+    spread_x(x0, 0, mats[0], mats[1])
+    spread_x(x1, 0, mats[2], mats[3])
+    y_bands = jnp.concatenate([y0[0], y1[0]], axis=0)
+
+    def emit(v, half, own_cells, ext):
+        blurred[v, :, half * rows : (half + 1) * rows, : own * LANES] = own_cells
+        blurred[v, :, half * rows : (half + 1) * rows, own * LANES :] = ext
+
+    forward(field, z_taps, y_bands, ((mats[0], mats[1]), (mats[2], mats[3])), inner, outer, emit)
+
+
+def fill_observed(meta, obs_own, obs_other, halo_a, halo_b, obs, rows, own, depth):
+    view = meta[0]
+    near = rows // 2
+    count = obs_own.shape[0]
+    at_a = pl.multiple_of(jnp.where(meta[1] == 1, rows + near, 0), near)
+    at_b = pl.multiple_of(jnp.where(meta[1] == 1, 0, rows + near), near)
+    for which, middle in enumerate((obs_own, obs_other)):
+        slot = jnp.where(view == 0, which, 1 - which)
+
+        def store(z, place, cells):
+            obs[slot, z, near : near + rows, place * LANES : (place + 1) * LANES] = cells
+
+        unpack_window(view, lambda n: middle[n], depth, own, 2, store)
+        for halo, at in ((halo_a, at_a), (halo_b, at_b)):
+
+            def store_halo(z, place, cells):
+                obs[slot, z, pl.ds(at, near), place * LANES : (place + 1) * LANES] = cells
+
+            unpack_window(view, lambda n: halo[which * count + n], depth, own, 2, store_halo)
+
+
+def row_mask(meta, rows, lanes):
+    at = lax.broadcasted_iota(jnp.int32, (2 * rows, lanes), 0)
+    low = jnp.where(meta[2] == 1, rows // 2, 0)
+    high = jnp.where(meta[3] == 1, rows + rows // 2, 2 * rows)
+    return (at >= low) & (at < high)
+
+
+def first_back_kernel(
+    meta, z_taps, est, blurred, obs_own, obs_other, halo_a, halo_b, y0, y1, x0, x1,
+    obs, current, to_send, ratio, inner, outer, *mats
+):
+    depth, rows, width = est.shape
+    own = width // LANES // 2
+    lanes = (own + 1) * LANES
+    view = meta[0]
+    fill_observed(meta, obs_own, obs_other, halo_a, halo_b, obs, rows, own, depth)
+    spread_x(x0, 1, mats[0], mats[1])
+    spread_x(x1, 1, mats[2], mats[3])
+    inside = row_mask(meta, rows, lanes)
+    gains = []
+    for v in range(2):
+        for z in range(depth):
+            ratio[z] = jnp.where(inside, obs[v, z] / blurred[v, z], 0.0)
+        y_band = (y0, y1)[v][1]
+        gains.append(backward(ratio, v, z_taps, y_band, mats[2 * v : 2 * v + 2], inner, outer))
+    root_own = jnp.sqrt(gains[0][0] * gains[1][0])
+    root_ext = jnp.sqrt(gains[0][1] * gains[1][1])
+    for place in range(own + 1):
+        cells = est[:, :, block_at(view, place, width // LANES)]
+        factor = root_ext if place == own else root_own[:, :, place * LANES : (place + 1) * LANES]
+        current[:, :, place * LANES : (place + 1) * LANES] = cells * factor
+    pack_window(
+        view, lambda z, p: current[z, :, p * LANES : (p + 1) * LANES], depth, own, 4, to_send
+    )
+
+
+def second_kernel(
+    meta, z_taps, current, got_a, got_b, obs, y0, y1, x0, x1,
+    out, field, ratios, inner, outer, *mats
+):
+    depth, rows, lanes = current.shape
+    own = lanes // LANES - 1
+    view = meta[0]
+    field[:, rows : 2 * rows, :] = current[...]
+    for got, at in zip((got_a, got_b), place_rows(meta[1], rows)):
+
+        def store(z, place, cells, at=at):
+            field[z, pl.ds(at, rows), place * LANES : (place + 1) * LANES] = cells
+
+        unpack_window(view, lambda n, got=got: got[n], depth, own, 4, store)
+    spread_x(x0, 0, mats[0], mats[1])
+    spread_x(x1, 0, mats[2], mats[3])
+    spread_x(x0, 1, mats[4], None)
+    spread_x(x1, 1, mats[5], None)
+    y_bands = jnp.concatenate([y0[0], y1[0]], axis=0)
+    inside = row_mask(meta, rows, LANES)
+
+    def emit(v, half, own_cells, ext):
+        at = slice(half * rows, (half + 1) * rows)
+        mask = inside[at]
+        for place in range(own + 1):
+            cols = slice(place * LANES, (place + 1) * LANES)
+            cells = ext if place == own else own_cells[:, :, cols]
+            ratios[v, :, at, cols] = jnp.where(mask[None], obs[v, :, at, cols] / cells, 0.0)
+
+    forward(field, z_taps, y_bands, ((mats[0], mats[1]), (mats[2], mats[3])), inner, outer, emit)
+    gains = []
+    for v in range(2):
+        y_band = (y0, y1)[v][1]
+        gains.append(
+            backward(ratios.at[v], v, z_taps, y_band, (mats[4 + v], None), inner, outer)[0]
+        )
+    result = current[:, :, : own * LANES] * jnp.sqrt(gains[0] * gains[1])
+    for place in range(own):
+        at = jnp.where(view == 0, place, own - 1 - place)
+        out[:, :, pl.ds(pl.multiple_of(at * LANES, LANES), LANES)] = result[
+            :, :, place * LANES : (place + 1) * LANES
+        ]
+
+
+def paired(cells_a, cells_b):
+    count = lax.axis_size("tile")
+    pairs_a = [(i, i ^ 1) for i in range(count)]
+    pairs_b = []
+    for i in range(1, count - 1, 2):
+        pairs_b += [(i, i + 1), (i + 1, i)]
+    got_b = lax.ppermute(cells_b, "tile", pairs_b)
+    got_a = lax.ppermute(cells_a, "tile", pairs_a)
+    return got_a, got_b
+
+
+def two_view_body(estimate, observed, psf_taps):
+    depth, rows, width = estimate.shape
+    blocks = width // LANES
+    own = blocks // 2
+    lanes = (own + 1) * LANES
+    length = psf_taps.shape[2]
+    view = lax.axis_index("view")
+    tile = lax.axis_index("tile")
+    last = lax.axis_size("tile") - 1
+    even = 1 - lax.rem(tile, 2)
+    swap = [(0, 1), (1, 0)]
+    meta = jnp.stack([view, even, tile == 0, tile == last]).astype(jnp.int32)
+    count = own * depth + depth // 2
+    count_mid = own * depth + depth // 4
+
+    other_taps = lax.ppermute(psf_taps, "view", swap)
+    est_send = pl.pallas_call(
+        est_pack_kernel, out_shape=shaped((count, rows, LANES)), in_specs=[SMEM, VMEM],
+        out_specs=VMEM, name="est_pack",
+    )(meta, estimate)
+    est_a, est_b = paired(est_send, est_send)
+    mine, theirs = pl.pallas_call(
+        obs_pack_kernel, out_shape=[shaped((count, rows, LANES))] * 2, in_specs=[SMEM, VMEM],
+        out_specs=[VMEM, VMEM], name="obs_pack",
+    )(meta, observed)
+    other = lax.ppermute(theirs, "view", swap)
+    both = jnp.concatenate([mine, other], axis=0)
+    near = rows // 2
+    halo_a, halo_b = paired(
+        lax.dynamic_slice_in_dim(both, even * near, near, 1),
+        lax.dynamic_slice_in_dim(both, (1 - even) * near, near, 1),
+    )
+
+    taps = jnp.where(
+        view == 0,
+        jnp.concatenate([psf_taps, other_taps], axis=0),
+        jnp.concatenate([other_taps, psf_taps], axis=0),
+    )
+    normed = taps / jnp.sum(taps, axis=2, keepdims=True)
+    z_taps = normed[:, 0]
+    bands = [
+        pl.pallas_call(
+            bands_kernel,
+            out_shape=[shaped((2, rows, 6 * rows), BF), shaped((2, 2, 3 * LANES, LANES), BF)],
+            in_specs=[SMEM, SMEM], out_specs=[VMEM, VMEM], name="bands",
+        )(meta, normed[v])
+        for v in range(2)
+    ]
+    mats = [bands[0][0], bands[1][0], bands[0][1], bands[1][1]]
+    own_mat = pltpu.VMEM((3 * lanes, own * LANES), BF)
+    ext_mat = pltpu.VMEM((6 * LANES, LANES), BF)
+    inner = pltpu.VMEM((depth, 2 * rows, lanes), F32)
+    outer = pltpu.VMEM((depth, rows, lanes), F32)
+
+    blurred = pl.pallas_call(
+        forward_kernel, out_shape=shaped((2, depth, 2 * rows, lanes)),
+        in_specs=[SMEM, SMEM] + [VMEM] * 7, out_specs=VMEM,
+        scratch_shapes=[pltpu.VMEM((depth, 3 * rows, lanes), F32), inner, outer] + [own_mat, ext_mat] * 2,
+        name="first_forward",
+    )(meta, z_taps, estimate, est_a, est_b, *mats)
+    obs, current, cur_send = pl.pallas_call(
+        first_back_kernel,
+        out_shape=[
+            shaped((2, depth, 2 * rows, lanes)), shaped((depth, rows, lanes)), shaped((count_mid, rows, LANES)),
+        ],
+        in_specs=[SMEM, SMEM] + [VMEM] * 10, out_specs=[VMEM] * 3,
+        scratch_shapes=[pltpu.VMEM((depth, 2 * rows, lanes), F32), inner, outer] + [own_mat, ext_mat] * 2,
+        name="first_back",
+    )(meta, z_taps, estimate, blurred, mine, other, halo_a, halo_b, *mats)
+    cur_a, cur_b = paired(cur_send, cur_send)
+    half = pl.pallas_call(
+        second_kernel, out_shape=shaped((depth, rows, own * LANES)),
+        in_specs=[SMEM, SMEM] + [VMEM] * 8, out_specs=VMEM,
+        scratch_shapes=[
+            pltpu.VMEM((depth, 3 * rows, lanes), F32), pltpu.VMEM((2, depth, 2 * rows, lanes), F32),
+            inner, outer,
+        ] + [own_mat, ext_mat] * 2 + [own_mat] * 2,
+        name="second",
+    )(meta, z_taps, current, cur_a, cur_b, obs, *mats)
+    far = lax.ppermute(half, "view", swap)
+    return jnp.where(
+        view == 0, jnp.concatenate([half, far], axis=2), jnp.concatenate([far, half], axis=2)
+    )
 
 
 def extended_2(cells, sides, width):
@@ -80,8 +492,29 @@
     return current
 
 
+def fits(mesh, estimate, psf_taps):
+    depth, rows, width = estimate.shape
+    tiles = mesh.shape["tile"]
+    reach = (psf_taps.shape[2] - 1) // 2
+    return (
+        mesh.shape["view"] == 2
+        and tiles % 2 == 0
+        and rows % (32 * tiles) == 0
+        and rows // tiles >= 2 * (reach + 1)
+        and width % (2 * LANES) == 0
+        and 4 * reach <= LANES // 2
+        and 2 * reach <= LANES // 4
+        and depth % 4 == 0
+    )
+
+
 def solution(mesh):
     placed = (P(None, "tile", None), P("view", None, "tile", None), P("view", None, None))
-    return jax.shard_map(
-        body, mesh=mesh, in_specs=placed, out_specs=P(None, "tile", None), check_vma=False
-    )
+
+    def run(estimate, observed, psf_taps):
+        chosen = two_view_body if fits(mesh, estimate, psf_taps) else body
+        return jax.shard_map(
+            chosen, mesh=mesh, in_specs=placed, out_specs=P(None, "tile", None), check_vma=False
+        )(estimate, observed, psf_taps)
+
+    return run

time: 233 us -> 68.3 us (0.29)
  local copies, waits for them, and re-layouts: 111 us -> 5.35 us
  starting transfers between devices: 44.1 us -> 13.8 us
  Pallas kernels: 0 us -> 24.1 us
  matrix products: 18.9 us -> 0 us
  blocking collectives: 15.2 us -> 0 us
  waiting for transfers between devices: 33.4 us -> 22 us
  other arithmetic: 8.52 us -> 2.67 us
    gather x12 -> x0, local copies, waits for them, and re-layouts: 101 us -> none  [band_matrix(): return jnp.where(inside, jnp.take(taps, jnp.clip(lag, 0, length - 1)), 0.0)]
    ppermute x16 -> x9, starting transfers between devices: 40.1 us -> 13.8 us  [the longest x3 11.8 us: paired(): got_b = lax.ppermute(cells_b, 'tile', pairs_b)]
    pallas_call x0 -> x7, Pallas kernels: none -> 24.1 us  [the longest x1 6.45 us: two_view_body(): pl.pallas_call(second_kernel, out_shape=shaped((depth, rows, own * LANES)...]
    dot_general x16 -> x0, matrix products: 18.9 us -> none  [the longest x8 6.3 us: blur(): jnp.einsum('vzyj,vjx->vzyx', piece, x_mats, precision=highest)]
    all_gather x2 -> x0, blocking collectives: 15.2 us -> none  [the longest x1 7.85 us: body(): taps = lax.all_gather(psf_taps, 'view', axis=0, tiled=True)]
    ppermute x16 -> x9, waiting for transfers between devices: 33.4 us -> 22 us  [the longest x3 7.83 us: paired(): got_b = lax.ppermute(cells_b, 'tile', pairs_b)]
    all_to_all x1 -> x0, starting transfers between devices: 3.98 us -> none  [body(): lax.all_to_all(observed, 'view', split_axis=3, concat_axis=0, tiled=True)]
    concatenate x4 -> x0, other arithmetic: 2.68 us -> none  [extended_2(): jnp.concatenate([lax.ppermute(tail, axis, [(i, (i + 1) % count) for i in...]
  transfers between devices with their start and end apart: 17 -> 9, of which waited for: 10 -> 3; matrix products, arithmetic and copies ran while one was open for 49% -> 4% of each run, Pallas kernels for 0% -> 16%
where the time goes in v1:
time: 68.3 us; the launch traced here: 68 us
  Pallas kernels  24.1 us (35%)
  waiting for transfers between devices  22 us (32%)
  starting transfers between devices  13.8 us (20%)
  local copies, waits for them, and re-layouts  5.35 us (8%)
  other arithmetic  2.67 us (4%)
    ppermute x3, starting transfers between devices, paired(): got_b = lax.ppermute(cells_b, 'tile', pairs_b)  11.8 us
    ppermute x3, waiting for transfers between devices, paired(): got_b = lax.ppermute(cells_b, 'tile', pairs_b)  7.83 us
    ppermute x1, waiting for transfers between devices, two_view_body(): other = lax.ppermute(theirs, 'view', swap)  7.32 us
    ppermute x1, waiting for transfers between devices, two_view_body(): far = lax.ppermute(half, 'view', swap)  6.81 us
    pallas_call x1, Pallas kernels, two_view_body(): pl.pallas_call(second_kernel, out_shape=shaped((depth, rows, own * LANES)...  6.45 us
    pallas_call x1, Pallas kernels, two_view_body(): pl.pallas_call(forward_kernel, out_shape=shaped((2, depth, 2 * rows, lane...  4.96 us
    pallas_call x1, Pallas kernels, two_view_body(): pl.pallas_call(first_back_kernel, out_shape=[shaped((2, depth, 2 * rows,...  4.83 us
    unnamed x18, local copies, waits for them, and re-layouts  4.67 us
  transfers between devices with their start and end apart: 9, of which 3 were waited for; matrix products, arithmetic and copies ran while one was open for 4% of the time, Pallas kernels for 16%

profile of v1, /device:TPU:9, one launch (start us, length us, event | category | flops | bytes accessed | tf_op | source)
XLA Modules:
  0.0 68.0 jit_solution(8074707782705989038)
XLA Ops:
  0.0 0.6 pad_add_fusion.meta
  0.6 1.9 %est_pack.1 = f32[20,32,128]{2,1,0:T(8,128)} custom-call(s32[4]{0:T(128)} %pad_add_fusion.meta, f32[8,32,512]{2,1,0:T(8,128)} %est.5), custom_call_target="tpu_custom_call" | custom-call | tf_op jit(solution)/shard_map/est_pack/pallas_call | solution.py:352
  2.5 3.7 %collective-permute-start.2 = (f32[20,32,128]{2,1,0:T(8,128)}, f32[20,32,128]{2,1,0:T(8,128)S(1)}, u32[]{:S(2)}, u32[]{:S(2)}) collective-permute-start(f32[20,32,128]{2,1,0:T(8,128)} %est_pack.1), channel_id=1, source_target_pairs={{1,2},{2,1},{3,4},{4,3},{5,6},{6,5},{7,8},{8,7},{9,10},{10,9},{11,... | collective-permute-start | bytes 983048 | tf_op jit(solution)/shard_map/ppermute | solution.py:331
  6.2 1.3 %collective-permute-start = (f32[1,3,31]{2,0,1:T(1,128)}, f32[1,3,31]{2,0,1:T(1,128)S(1)}, u32[]{:S(2)}, u32[]{:S(2)}) collective-permute-start(f32[1,3,31]{2,0,1:T(1,128)} %param.5), channel_id=1, source_target_pairs={{0,16},{16,0},{1,17},{17,1},{2,18},{18,2},{3,19},{19,3},{4,20},{20... | collective-permute-start | bytes 1124 | tf_op jit(solution)/shard_map/ppermute | solution.py:351
  7.6 2.0 %obs_pack.1 = (f32[20,32,128]{2,1,0:T(8,128)}, f32[20,32,128]{2,1,0:T(8,128)}) custom-call(s32[4]{0:T(128)} %pad_add_fusion.meta, f32[1,8,32,512]{3,2,1,0:T(8,128)} %obs.1), custom_call_target="tpu_custom_call" | custom-call | tf_op jit(solution)/shard_map/obs_pack/pallas_call | solution.py:357
  9.8 1.0 %constant_dynamic-update-slice_fusion.1 = f32[40,32,128]{2,1,0:T(8,128)S(1)} fusion(f32[20,32,128]{2,1,0:T(8,128)} %get-tuple-element.18.obs_own), kind=kLoop, calls=%fused_computation.2 | loop fusion | bytes 655360
  11.0 7.3 %collective-permute-done.3.obs_other = f32[20,32,128]{2,1,0:T(8,128)S(1)} collective-permute-done((f32[20,32,128]{2,1,0:T(8,128)}, f32[20,32,128]{2,1,0:T(8,128)S(1)}, u32[]{:S(2)}, u32[]{:S(2)}) %collective-permute-start.3) | collective-permute-done | bytes 327712 | tf_op jit(solution)/shard_map/ppermute | solution.py:361
  18.4 4.6 %collective-permute-start.5 = (f32[40,16,128]{2,1,0:T(8,128)S(1)}, f32[40,16,128]{2,1,0:T(8,128)S(1)}, u32[]{:S(2)}, u32[]{:S(2)}) collective-permute-start(f32[40,16,128]{2,1,0:T(8,128)S(1)} %get-tuple-element.23), channel_id=1, source_target_pairs={{1,2},{2,1},{3,4},{4,3},{5,6},{6,5},{7,8},{8,7},{9,10},{10,9},{11,... | collective-permute-start | bytes 983048 | tf_op jit(solution)/shard_map/ppermute | solution.py:331
  23.1 0.6 copy_bitcast_fusion
  23.7 2.0 %bands.3 = (bf16[2,32,192]{2,1,0:T(8,128)(2,1)}, bf16[2,2,384,128]{3,2,1,0:T(8,128)(2,1)}) custom-call(s32[4]{0:T(128)} %pad_add_fusion.meta, f32[3,31]{1,0:T(4,128)} %get-tuple-element.27.taps), custom_call_target="tpu_custom_call" | custom-call | tf_op jit(solution)/shard_map/bands/pallas_call | solution.py:377
  25.7 2.0 %bands.2 = (bf16[2,32,192]{2,1,0:T(8,128)(2,1)}, bf16[2,2,384,128]{3,2,1,0:T(8,128)(2,1)}) custom-call(s32[4]{0:T(128)} %pad_add_fusion.meta, f32[3,31]{1,0:T(4,128)} %get-tuple-element.28.taps), custom_call_target="tpu_custom_call" | custom-call | tf_op jit(solution)/shard_map/bands/pallas_call | solution.py:377
  27.7 0.6 slice_bitcast_fusion.z_taps
  28.3 0.7 %copy-done.3 = f32[20,32,128]{2,1,0:T(8,128)} copy-done((f32[20,32,128]{2,1,0:T(8,128)}, f32[20,32,128]{2,1,0:T(8,128)S(1)}, u32[]{:S(2)}) %copy-start.3) | copy-done | bytes 327704
  29.1 5.0 %first_forward.1.blurred = f32[2,8,64,384]{3,2,1,0:T(8,128)} custom-call(s32[4]{0:T(128)} %pad_add_fusion.meta, f32[2,31]{1,0:T(2,128)} %slice_bitcast_fusion.z_taps, f32[8,32,512]{2,1,0:T(8,128)} %est.5, f32[20,32,128]{2,1,0:T(8,128)} %copy-done.4, f32[20,32,128]{2,1,0:T(8,128)} %copy-done.3, bf16[2,32,192]{2,1,0:T(8,128)(2,1)} %get-tuple-element.14.y0, ...), custom_call_target="tpu_custom_call" | custom-call | tf_op jit(solution)/shard_map/first_forward/pallas_call | solution.py:390
  34.1 0.7 %copy-done.1 = f32[40,16,128]{2,1,0:T(8,128)} copy-done((f32[40,16,128]{2,1,0:T(8,128)}, f32[40,16,128]{2,1,0:T(8,128)S(1)}, u32[]{:S(2)}) %copy-start.1) | copy-done | bytes 327704
  34.8 0.7 %copy-done.2 = f32[40,16,128]{2,1,0:T(8,128)} copy-done((f32[40,16,128]{2,1,0:T(8,128)}, f32[40,16,128]{2,1,0:T(8,128)S(1)}, u32[]{:S(2)}) %copy-start.2) | copy-done | bytes 327704
  35.5 4.8 %first_back.1 = (f32[2,8,64,384]{3,2,1,0:T(8,128)}, f32[8,32,384]{2,1,0:T(8,128)}, f32[18,32,128]{2,1,0:T(8,128)}) custom-call(s32[4]{0:T(128)} %pad_add_fusion.meta, f32[2,31]{1,0:T(2,128)} %slice_bitcast_fusion.z_taps, f32[8,32,512]{2,1,0:T(8,128)} %est.5, f32[2,8,64,384]{3,2,1,0:T(8,128)} %first_forward.1.blurred, ...), custom_call_target="tpu_custom_call" | custom-call | tf_op jit(solution)/shard_map/first_back/pallas_call | solution.py:396
  40.4 3.5 %collective-permute-start.7 = (f32[18,32,128]{2,1,0:T(8,128)}, f32[18,32,128]{2,1,0:T(8,128)S(1)}, u32[]{:S(2)}, u32[]{:S(2)}) collective-permute-start(f32[18,32,128]{2,1,0:T(8,128)} %get-tuple-element.21), channel_id=1, source_target_pairs={{1,2},{2,1},{3,4},{4,3},{5,6},{6,5},{7,8},{8,7},{9,10},{10,9},{11,... | collective-permute-start | bytes 884744 | tf_op jit(solution)/shard_map/ppermute | solution.py:331
  43.9 7.8 %collective-permute-done.7.got_b = f32[18,32,128]{2,1,0:T(8,128)S(1)} collective-permute-done((f32[18,32,128]{2,1,0:T(8,128)}, f32[18,32,128]{2,1,0:T(8,128)S(1)}, u32[]{:S(2)}, u32[]{:S(2)}) %collective-permute-start.7) | collective-permute-done | bytes 294944 | tf_op jit(solution)/shard_map/ppermute | solution.py:331
  51.8 0.7 %copy-done.5 = f32[18,32,128]{2,1,0:T(8,128)} copy-done((f32[18,32,128]{2,1,0:T(8,128)}, f32[18,32,128]{2,1,0:T(8,128)S(1)}, u32[]{:S(2)}) %copy-start.5) | copy-done | bytes 294936
  52.6 6.5 %second.1 = f32[8,32,256]{2,1,0:T(8,128)} custom-call(s32[4]{0:T(128)} %pad_add_fusion.meta, f32[2,31]{1,0:T(2,128)} %slice_bitcast_fusion.z_taps, f32[8,32,384]{2,1,0:T(8,128)} %get-tuple-element.20.current, f32[18,32,128]{2,1,0:T(8,128)} %copy-done.6, f32[18,32,128]{2,1,0:T(8,128)} %copy-done.5, f32[2,8,64,384]{3,2,1,0:T(8,128)} %get-tuple-element.22.obs, ...), custom_call_target="tpu_custom_call" | custom-call | tf_op jit(solution)/shard_map/second/pallas_call | solution.py:406
  59.0 0.2 collective-permute-start.8
  59.3 6.8 %collective-permute-done.8 = f32[8,32,256]{2,1,0:T(8,128)S(1)} collective-permute-done((f32[8,32,256]{2,1,0:T(8,128)}, f32[8,32,256]{2,1,0:T(8,128)S(1)}, u32[]{:S(2)}, u32[]{:S(2)}) %collective-permute-start.8) | collective-permute-done | bytes 262176 | tf_op jit(solution)/shard_map/ppermute | solution.py:415
  66.1 1.9 %maximum_select_fusion = f32[8,32,512]{2,1,0:T(8,128)} fusion(f32[8,32,256]{2,1,0:T(8,128)S(1)} %collective-permute-done.8, f32[8,32,256]{2,1,0:T(8,128)} %second.1, pred[]{:T(512)S(6)} %eq.10), kind=kLoop, calls=%fused_computation | loop fusion | flops 393216 | bytes 1048577 | tf_op jit(solution)/shard_map/jit(_where)/select_n | solution.py:416
  (27 shorter events, 1.0 us)
Async XLA Ops:
  0.0 10.8 %copy-start.7 = (f32[1,3,31]{2,0,1:T(1,128)S(1)}, f32[1,3,31]{2,0,1:T(1,128)}, u32[]{:S(2)}) copy-start(f32[1,3,31]{2,0,1:T(1,128)} %param.5) | copy-start | bytes 1120
  2.5 25.8 %collective-permute-start.2 = (f32[20,32,128]{2,1,0:T(8,128)}, f32[20,32,128]{2,1,0:T(8,128)S(1)}, u32[]{:S(2)}, u32[]{:S(2)}) collective-permute-start(f32[20,32,128]{2,1,0:T(8,128)} %est_pack.1), channel_id=1, source_target_pairs={{1,2},{2,1},{3,4},{4,3},{5,6},{6,5},{7,8},{8,7},{9,10},{10,9},{11,... | collective-permute-start | bytes 983048 | tf_op jit(solution)/shard_map/ppermute | solution.py:331
  6.2 22.1 %collective-permute-start.1 = (f32[20,32,128]{2,1,0:T(8,128)}, f32[20,32,128]{2,1,0:T(8,128)S(1)}, u32[]{:S(2)}, u32[]{:S(2)}) collective-permute-start(f32[20,32,128]{2,1,0:T(8,128)} %est_pack.1), channel_id=1, source_target_pairs={{0,1},{1,0},{2,3},{3,2},{4,5},{5,4},{6,7},{7,6},{8,9},{9,8},{10,11... | collective-permute-start | bytes 983048 | tf_op jit(solution)/shard_map/ppermute | solution.py:332
  6.2 4.5 %collective-permute-start = (f32[1,3,31]{2,0,1:T(1,128)}, f32[1,3,31]{2,0,1:T(1,128)S(1)}, u32[]{:S(2)}, u32[]{:S(2)}) collective-permute-start(f32[1,3,31]{2,0,1:T(1,128)} %param.5), channel_id=1, source_target_pairs={{0,16},{16,0},{1,17},{17,1},{2,18},{18,2},{3,19},{19,3},{4,20},{20... | collective-permute-start | bytes 1124 | tf_op jit(solution)/shard_map/ppermute | solution.py:351
  9.5 8.8 %collective-permute-start.3 = (f32[20,32,128]{2,1,0:T(8,128)}, f32[20,32,128]{2,1,0:T(8,128)S(1)}, u32[]{:S(2)}, u32[]{:S(2)}) collective-permute-start(f32[20,32,128]{2,1,0:T(8,128)} %get-tuple-element.19), channel_id=1, source_target_pairs={{0,16},{16,0},{1,17},{17,1},{2,18},{18,2},{3,19},{19,3},{4,20},{20... | collective-permute-start | bytes 983048 | tf_op jit(solution)/shard_map/ppermute | solution.py:361
  18.3 15.8 %copy-start = (f32[20,32,128]{2,1,0:T(8,128)}, f32[20,32,128]{2,1,0:T(8,128)S(1)}, u32[]{:S(2)}) copy-start(f32[20,32,128]{2,1,0:T(8,128)S(1)} %collective-permute-done.3.obs_other) | copy-start | bytes 983044
  18.4 15.7 %collective-permute-start.5 = (f32[40,16,128]{2,1,0:T(8,128)S(1)}, f32[40,16,128]{2,1,0:T(8,128)S(1)}, u32[]{:S(2)}, u32[]{:S(2)}) collective-permute-start(f32[40,16,128]{2,1,0:T(8,128)S(1)} %get-tuple-element.23), channel_id=1, source_target_pairs={{1,2},{2,1},{3,4},{4,3},{5,6},{6,5},{7,8},{8,7},{9,10},{10,9},{11,... | collective-permute-start | bytes 983048 | tf_op jit(solution)/shard_map/ppermute | solution.py:331
  23.0 11.0 %collective-permute-start.4 = (f32[40,16,128]{2,1,0:T(8,128)S(1)}, f32[40,16,128]{2,1,0:T(8,128)S(1)}, u32[]{:S(2)}, u32[]{:S(2)}) collective-permute-start(f32[40,16,128]{2,1,0:T(8,128)S(1)} %get-tuple-element.24), channel_id=1, source_target_pairs={{0,1},{1,0},{2,3},{3,2},{4,5},{5,4},{6,7},{7,6},{8,9},{9,8},{10,11... | collective-permute-start | bytes 983048 | tf_op jit(solution)/shard_map/ppermute | solution.py:332
  28.3 0.7 %copy-start.3 = (f32[20,32,128]{2,1,0:T(8,128)}, f32[20,32,128]{2,1,0:T(8,128)S(1)}, u32[]{:S(2)}) copy-start(f32[20,32,128]{2,1,0:T(8,128)S(1)} %collective-permute-done.2.got_b) | copy-start | bytes 983044
  28.3 0.8 %copy-start.4 = (f32[20,32,128]{2,1,0:T(8,128)}, f32[20,32,128]{2,1,0:T(8,128)S(1)}, u32[]{:S(2)}) copy-start(f32[20,32,128]{2,1,0:T(8,128)S(1)} %collective-permute-done.1.got_a) | copy-start | bytes 983044
  34.1 0.7 %copy-start.1 = (f32[40,16,128]{2,1,0:T(8,128)}, f32[40,16,128]{2,1,0:T(8,128)S(1)}, u32[]{:S(2)}) copy-start(f32[40,16,128]{2,1,0:T(8,128)S(1)} %collective-permute-done.5.halo_b) | copy-start | bytes 983044
  34.8 0.7 %copy-start.2 = (f32[40,16,128]{2,1,0:T(8,128)}, f32[40,16,128]{2,1,0:T(8,128)S(1)}, u32[]{:S(2)}) copy-start(f32[40,16,128]{2,1,0:T(8,128)S(1)} %collective-permute-done.4.halo_a) | copy-start | bytes 983044
  40.4 11.4 %collective-permute-start.7 = (f32[18,32,128]{2,1,0:T(8,128)}, f32[18,32,128]{2,1,0:T(8,128)S(1)}, u32[]{:S(2)}, u32[]{:S(2)}) collective-permute-start(f32[18,32,128]{2,1,0:T(8,128)} %get-tuple-element.21), channel_id=1, source_target_pairs={{1,2},{2,1},{3,4},{4,3},{5,6},{6,5},{7,8},{8,7},{9,10},{10,9},{11,... | collective-permute-start | bytes 884744 | tf_op jit(solution)/shard_map/ppermute | solution.py:331
  43.9 7.9 %collective-permute-start.6 = (f32[18,32,128]{2,1,0:T(8,128)}, f32[18,32,128]{2,1,0:T(8,128)S(1)}, u32[]{:S(2)}, u32[]{:S(2)}) collective-permute-start(f32[18,32,128]{2,1,0:T(8,128)} %get-tuple-element.21), channel_id=1, source_target_pairs={{0,1},{1,0},{2,3},{3,2},{4,5},{5,4},{6,7},{7,6},{8,9},{9,8},{10,11... | collective-permute-start | bytes 884744 | tf_op jit(solution)/shard_map/ppermute | solution.py:332
  51.8 0.7 %copy-start.5 = (f32[18,32,128]{2,1,0:T(8,128)}, f32[18,32,128]{2,1,0:T(8,128)S(1)}, u32[]{:S(2)}) copy-start(f32[18,32,128]{2,1,0:T(8,128)S(1)} %collective-permute-done.7.got_b) | copy-start | bytes 884740
  51.8 0.8 %copy-start.6 = (f32[18,32,128]{2,1,0:T(8,128)}, f32[18,32,128]{2,1,0:T(8,128)S(1)}, u32[]{:S(2)}) copy-start(f32[18,32,128]{2,1,0:T(8,128)S(1)} %collective-permute-done.6.got_a) | copy-start | bytes 884740
  59.0 7.0 %collective-permute-start.8 = (f32[8,32,256]{2,1,0:T(8,128)}, f32[8,32,256]{2,1,0:T(8,128)S(1)}, u32[]{:S(2)}, u32[]{:S(2)}) collective-permute-start(f32[8,32,256]{2,1,0:T(8,128)} %second.1), channel_id=1, source_target_pairs={{0,16},{16,0},{1,17},{17,1},{2,18},{18,2},{3,19},{19,3},{4,20},{20... | collective-permute-start | bytes 786440 | tf_op jit(solution)/shard_map/ppermute | solution.py:415

commit v2 on v0

--- a/solution.py
+++ b/solution.py
@@ -1,9 +1,485 @@
 import jax
 import jax.numpy as jnp
 from jax import lax
+from jax.experimental import pallas as pl
+from jax.experimental.pallas import tpu as pltpu
 from jax.sharding import PartitionSpec as P
 
+
 ITERS = 2
+LANES = 128
+VMEM_BYTES = 24 << 20
+BF = jnp.bfloat16
+F32 = jnp.float32
+VMEM = pl.BlockSpec(memory_space=pltpu.VMEM)
+SMEM = pl.BlockSpec(memory_space=pltpu.SMEM)
+HBM = pl.BlockSpec(memory_space=pltpu.HBM)
+
+
+def shaped(shape, dtype=F32):
+    return jax.ShapeDtypeStruct(shape, dtype)
+
+
+def call(kernel, outs, in_specs, out_specs=None, scratch=(), **more):
+    return pl.pallas_call(
+        kernel, out_shape=outs, in_specs=in_specs,
+        out_specs=out_specs or jax.tree.map(lambda _: VMEM, outs), scratch_shapes=scratch,
+        compiler_params=pltpu.CompilerParams(vmem_limit_bytes=VMEM_BYTES), **more,
+    )
+
+
+def in_hbm(cells):
+    return pltpu.with_memory_space_constraint(cells, pltpu.HBM)
+
+
+def split(cells):
+    high = cells.astype(BF)
+    return high, (cells - high.astype(F32)).astype(BF)
+
+
+def block_at(view, place, blocks):
+    at = jnp.where(view == 0, place, blocks - 1 - place)
+    return pl.ds(pl.multiple_of(at * LANES, LANES), LANES)
+
+
+def fold(planes, view, parts):
+    piece = LANES // parts
+    lane = lax.broadcasted_iota(jnp.int32, planes[0].shape, 1)
+    first = jnp.where(view == 0, 0, piece)
+    total = None
+    for at, plane in enumerate(planes):
+        moved = pltpu.roll(plane, lax.rem(first + at * piece, LANES), 1)
+        total = moved if total is None else jnp.where(lane >= at * piece, moved, total)
+    return total
+
+
+def unfold(folded, view, parts, at):
+    piece = LANES // parts
+    first = jnp.where(view == 0, LANES, LANES - piece)
+    return pltpu.roll(folded, lax.rem(first - at * piece, LANES), 1)
+
+
+def pack_window(view, planes_of, depth, own, parts, out_ref):
+    for place in range(own):
+        for z in range(depth):
+            out_ref[place * depth + z] = planes_of(z, place)
+    for group in range(depth // parts):
+        planes = [planes_of(group * parts + at, own) for at in range(parts)]
+        out_ref[own * depth + group] = fold(planes, view, parts)
+
+
+def unpack_window(view, packed_of, depth, own, parts, store):
+    for place in range(own):
+        for z in range(depth):
+            store(z, place, packed_of(place * depth + z))
+    for group in range(depth // parts):
+        folded = packed_of(own * depth + group)
+        for at in range(parts):
+            store(group * parts + at, own, unfold(folded, view, parts, at))
+
+
+def load_kernel(meta, obs_hbm, est_hbm, taps, obs, est, theirs, obs_sems, est_sem):
+    _, depth, _, width = obs.shape
+    own = width // LANES // 2
+    view = 1 - meta[0]
+    copies = [
+        pltpu.make_async_copy(obs_hbm.at[:, pl.ds(z, 1)], obs.at[:, pl.ds(z, 1)], obs_sems.at[z])
+        for z in range(depth)
+    ]
+    for copy in copies:
+        copy.start()
+    est_copy = pltpu.make_async_copy(est_hbm, est, est_sem)
+    est_copy.start()
+    _, kinds, length = taps.shape
+    theirs[own * depth + depth // 2] = jnp.zeros_like(theirs[0])
+    theirs[own * depth + depth // 2, :kinds, :length] = taps[0]
+    for z in range(0, depth, 2):
+        copies[z].wait()
+        copies[z + 1].wait()
+        for at in (z, z + 1):
+            for place in range(own):
+                theirs[place * depth + at] = obs[0, at, :, block_at(view, place, width // LANES)]
+        ends = [obs[0, at, :, block_at(view, own, width // LANES)] for at in (z, z + 1)]
+        theirs[own * depth + z // 2] = fold(ends, view, 2)
+    est_copy.wait()
+
+
+def near_rows(even, rows):
+    near = rows // 2
+    at_a = pl.multiple_of(jnp.where(even == 1, near, 0), near)
+    at_b = pl.multiple_of(jnp.where(even == 1, 0, near), near)
+    return at_a, at_b
+
+
+def pack_kernel(meta, est, send):
+    depth, _, width = est.shape
+    blocks = width // LANES
+    pack_window(
+        meta[0], lambda z, p: est[z, :, block_at(meta[0], p, blocks)], depth, blocks // 2, 2, send
+    )
+
+
+def pack_near_kernel(meta, obs, send_a, send_b):
+    _, depth, rows, width = obs.shape
+    blocks = width // LANES
+    near = rows // 2
+    for send, at in zip((send_a, send_b), near_rows(meta[1], rows)):
+        pack_window(
+            meta[0],
+            lambda z, p, at=at: obs[0, z, pl.ds(at, near), block_at(meta[0], p, blocks)],
+            depth, blocks // 2, 2, send,
+        )
+
+
+def bands_kernel(meta, taps, y_out, own_mats, ext_mats, band):
+    length = taps.shape[2]
+    reach = (length - 1) // 2
+    rows = y_out.shape[2]
+    span = 2 * rows
+    low = (LANES - reach) // 16 * 16
+    high = -(-(2 * LANES + reach) // 16) * 16
+    before, after = LANES - low, high - 2 * LANES
+    at_before = pl.multiple_of(jnp.where(meta[0] == 0, low, 2 * LANES + low), 16)
+    at_after = pl.multiple_of(jnp.where(meta[0] == 0, 2 * LANES, 0), 16)
+    lag = (
+        lax.broadcasted_iota(jnp.int32, (high - low, LANES), 0)
+        + (low - LANES)
+        - lax.broadcasted_iota(jnp.int32, (high - low, LANES), 1)
+    )
+    r_at = lax.broadcasted_iota(jnp.int32, (rows, 3 * span), 0)
+    s_at = lax.broadcasted_iota(jnp.int32, (rows, 3 * span), 1)
+    y_lag = lax.rem(s_at, span) - r_at - rows // 2
+    band[...] = jnp.zeros_like(band)
+    for view in range(2):
+        for back in range(2):
+            x_band = jnp.zeros(lag.shape, F32)
+            y_band = jnp.zeros(y_lag.shape, F32)
+            for tap in range(length):
+                at = tap - reach if back == 0 else reach - tap
+                x_band = jnp.where(lag == at, taps[view, 2, tap], x_band)
+                y_band = jnp.where(y_lag == at, taps[view, 1, tap], y_band)
+            for which, cells in enumerate(split(x_band)):
+                band[which, pl.ds(at_before, before)] = cells[:before]
+                band[which, LANES : 2 * LANES] = cells[before : before + LANES]
+                band[which, pl.ds(at_after, after)] = cells[before + LANES :]
+            spread_x(band, own_mats.at[view, back], ext_mats.at[view, back])
+            y_high = y_band.astype(BF).astype(F32)
+            y_out[view, back] = jnp.where(s_at < 2 * span, y_high, y_band - y_high).astype(BF)
+
+
+def spread_x(band, own_mat, ext_mat):
+    own = own_mat.shape[1] // LANES
+    for part, which in enumerate((0, 1, 0)):
+        for src in range(own + 1):
+            at = (part * (own + 1) + src) * LANES
+            for dst in range(own):
+                if abs(src - dst) <= 1:
+                    start = (src - dst + 1) * LANES
+                    cells = band[which, start : start + LANES, :]
+                else:
+                    cells = jnp.zeros((LANES, LANES), BF)
+                own_mat[at : at + LANES, dst * LANES : (dst + 1) * LANES] = cells
+        for src in range(2):
+            at = (part * 2 + src) * LANES
+            ext_mat[at : at + LANES, :] = band[which, src * LANES : (src + 1) * LANES, :]
+
+
+def y_stage(source, bands):
+    high, low = split(source)
+    return jnp.dot(bands, jnp.concatenate([high, low, high], axis=0), preferred_element_type=F32)
+
+
+def z_stage(taps, view, back, inner, base, rows, outer):
+    depth = inner.shape[0]
+    reach = (taps.shape[1] - 1) // 2
+    for row in range(0, rows, 8):
+        planes = [inner[z, base + row : base + row + 8, :] for z in range(depth)]
+        for out in range(depth):
+            total = None
+            for z in range(depth):
+                at = reach + (out - z if back else z - out)
+                term = taps[view, at] * planes[z]
+                total = term if total is None else total + term
+            outer[out, row : row + 8, :] = total
+
+
+def x_stage(cells, own_mat, ext_mat):
+    depth, rows, lanes = cells.shape
+    flat = cells.reshape(depth * rows, lanes)
+    high, low = split(flat)
+    left = jnp.concatenate([high, high, low], axis=1)
+    own = jnp.dot(left, own_mat[...], preferred_element_type=F32).reshape(depth, rows, -1)
+    if ext_mat is None:
+        return own, None
+    at = lanes - 2 * LANES
+    left = jnp.concatenate([high[:, at:], high[:, at:], low[:, at:]], axis=1)
+    ext = jnp.dot(left, ext_mat[...], preferred_element_type=F32).reshape(depth, rows, LANES)
+    return own, ext
+
+
+def forward(field, z_taps, y_bands, own_mats, ext_mats, inner, outer, emit):
+    depth = field.shape[0]
+    rows = outer.shape[2]
+    both = jnp.concatenate([y_bands[0, 0], y_bands[1, 0]], axis=0)
+    for half in range(2):
+        for z in range(depth):
+            inner[half, z] = y_stage(field[z, half * rows : half * rows + 2 * rows, :], both)
+        for view in range(2):
+            z_stage(z_taps, view, False, inner.at[half], view * rows, rows, outer.at[view])
+            emit(view, half, *x_stage(outer[view], own_mats.at[view, 0], ext_mats.at[view, 0]))
+
+
+def backward(ratio, view, z_taps, y_bands, own_mats, ext_mats, inner, outer):
+    depth = ratio.shape[0]
+    rows = outer.shape[2]
+    for z in range(depth):
+        inner[view, z, :rows, :] = y_stage(ratio[z], y_bands[view, 1])
+    z_stage(z_taps, view, True, inner.at[view], 0, rows, outer.at[view])
+    ext_mat = None if ext_mats is None else ext_mats.at[view, 1]
+    return x_stage(outer[view], own_mats.at[view, 1], ext_mat)
+
+
+def block_rows(even, rows):
+    at_a = pl.multiple_of(jnp.where(even == 1, 2 * rows, 0), rows)
+    at_b = pl.multiple_of(jnp.where(even == 1, 0, 2 * rows), rows)
+    return at_a, at_b
+
+
+def halo_rows(even, rows):
+    near = rows // 2
+    at_a = pl.multiple_of(jnp.where(even == 1, rows + near, 0), near)
+    at_b = pl.multiple_of(jnp.where(even == 1, 0, rows + near), near)
+    return at_a, at_b
+
+
+def cols(place):
+    return slice(place * LANES, (place + 1) * LANES)
+
+
+def row_mask(meta, rows, lanes):
+    at = lax.broadcasted_iota(jnp.int32, (2 * rows, lanes), 0)
+    low = jnp.where(meta[2] == 1, rows // 2, 0)
+    high = jnp.where(meta[3] == 1, rows + rows // 2, 2 * rows)
+    return (at >= low) & (at < high)
+
+
+def first_kernel(
+    meta, z_taps, est, obs_own, got_a, got_b, own_a, own_b, other, y_bands, own_mats, ext_mats,
+    obs, ratio, gain, field, inner, outer
+):
+    depth, rows, width = est.shape
+    own = width // LANES // 2
+    view = meta[0]
+    near = rows // 2
+    mid = slice(near, near + rows)
+    for place in range(own + 1):
+        from_lanes = block_at(view, place, width // LANES)
+        field[:, rows : 2 * rows, cols(place)] = est[:, :, from_lanes]
+        obs[0, :, mid, cols(place)] = obs_own[0, :, :, from_lanes]
+
+    def store_other(z, place, cells):
+        obs[1, z, mid, cols(place)] = cells
+
+    unpack_window(view, lambda n: other[n], depth, own, 2, store_other)
+    ends = zip(
+        (got_a, got_b), (own_a, own_b), block_rows(meta[1], rows), halo_rows(meta[1], rows)
+    )
+    for got, got_halo, at, at_halo in ends:
+
+        def store(z, place, cells, at=at):
+            field[z, pl.ds(at, rows), cols(place)] = cells
+
+        def store_halo(z, place, cells, at=at_halo):
+            obs[0, z, pl.ds(at, near), cols(place)] = cells
+
+        unpack_window(view, lambda n, got=got: got[n], depth, own, 2, store)
+        unpack_window(view, lambda n, got=got_halo: got[n], depth, own, 2, store_halo)
+    inside = row_mask(meta, rows, LANES)
+
+    def emit(v, half, own_cells, ext):
+        at = slice(half * rows, (half + 1) * rows)
+        for place in range(own + 1):
+            cells = ext if place == own else own_cells[:, :, cols(place)]
+            if v == 0:
+                mask = inside[at]
+                ratio[0, :, at, cols(place)] = jnp.where(
+                    mask[None], obs[0, :, at, cols(place)] / cells, 0.0
+                )
+            else:
+                halo = slice(0, near) if half == 0 else slice(near, rows)
+                keep = slice(near, rows) if half == 0 else slice(0, near)
+                base = half * rows
+                halo_at = slice(base + halo.start, base + halo.stop)
+                keep_at = slice(base + keep.start, base + keep.stop)
+                ratio[1, :, halo_at, cols(place)] = cells[:, halo]
+                ratio[1, :, keep_at, cols(place)] = obs[1, :, keep_at, cols(place)] / cells[:, keep]
+
+    forward(field, z_taps, y_bands, own_mats, ext_mats, inner, outer, emit)
+    back = backward(ratio.at[0], 0, z_taps, y_bands, own_mats, ext_mats, inner, outer)
+    gain[:, :, : own * LANES] = back[0]
+    gain[:, :, own * LANES :] = back[1]
+
+
+def update_kernel(
+    meta, z_taps, est, gain, obs_in, ratio_in, halo_a, halo_b, y_bands, own_mats, ext_mats,
+    obs, ratio, current, to_send, inner, outer
+):
+    depth, rows, width = est.shape
+    own = width // LANES // 2
+    view = meta[0]
+    near = rows // 2
+    for halo, at in zip((halo_a, halo_b), halo_rows(meta[1], rows)):
+        known = jnp.where(at == 0, 1 - meta[2], 1 - meta[3]) == 1
+
+        def store(z, place, cells, at=at, known=known):
+            obs[1, z, pl.ds(at, near), cols(place)] = cells
+            blurred = ratio_in[1, z, pl.ds(at, near), cols(place)]
+            ratio[1, z, pl.ds(at, near), cols(place)] = jnp.where(known, cells / blurred, 0.0)
+
+        unpack_window(view, lambda n, halo=halo: halo[n], depth, own, 2, store)
+    back = backward(ratio.at[1], 1, z_taps, y_bands, own_mats, ext_mats, inner, outer)
+    for place in range(own + 1):
+        cells = est[:, :, block_at(view, place, width // LANES)]
+        other = back[1] if place == own else back[0][:, :, cols(place)]
+        current[:, :, cols(place)] = cells * jnp.sqrt(gain[:, :, cols(place)] * other)
+    pack_window(view, lambda z, p: current[z, :, cols(p)], depth, own, 4, to_send)
+
+
+def second_kernel(
+    meta, z_taps, current, got_a, got_b, obs, y_bands, own_mats, ext_mats,
+    out, field, ratios, inner, outer
+):
+    depth, rows, lanes = current.shape
+    own = lanes // LANES - 1
+    view = meta[0]
+    field[:, rows : 2 * rows, :] = current[...]
+    for got, at in zip((got_a, got_b), block_rows(meta[1], rows)):
+
+        def store(z, place, cells, at=at):
+            field[z, pl.ds(at, rows), cols(place)] = cells
+
+        unpack_window(view, lambda n, got=got: got[n], depth, own, 4, store)
+    inside = row_mask(meta, rows, LANES)
+
+    def emit(v, half, own_cells, ext):
+        at = slice(half * rows, (half + 1) * rows)
+        mask = inside[at]
+        for place in range(own + 1):
+            cells = ext if place == own else own_cells[:, :, cols(place)]
+            ratios[v, :, at, cols(place)] = jnp.where(
+                mask[None], obs[v, :, at, cols(place)] / cells, 0.0
+            )
+
+    forward(field, z_taps, y_bands, own_mats, ext_mats, inner, outer, emit)
+    gains = [
+        backward(ratios.at[v], v, z_taps, y_bands, own_mats, None, inner, outer)[0]
+        for v in range(2)
+    ]
+    result = current[:, :, : own * LANES] * jnp.sqrt(gains[0] * gains[1])
+    for place in range(own):
+        at = jnp.where(view == 0, place, own - 1 - place)
+        out[:, :, pl.ds(pl.multiple_of(at * LANES, LANES), LANES)] = result[:, :, cols(place)]
+
+
+def copy_planes(cells, out, at, sems):
+    width = cells.shape[2]
+    copies = [
+        pltpu.make_async_copy(cells.at[z], out.at[z, :, pl.ds(at, width)], sems.at[z])
+        for z in range(cells.shape[0])
+    ]
+    for copy in copies:
+        copy.start()
+    for copy in copies:
+        copy.wait()
+
+
+def place_kernel(meta, half, out, sems):
+    width = half.shape[2]
+    copy_planes(half, out, pl.multiple_of(meta[0] * width, width), sems)
+
+
+def paired(cells_a, cells_b):
+    count = lax.axis_size("tile")
+    pairs_a = [(i, i ^ 1) for i in range(count)]
+    pairs_b = []
+    for i in range(1, count - 1, 2):
+        pairs_b += [(i, i + 1), (i + 1, i)]
+    got_b = lax.ppermute(cells_b, "tile", pairs_b)
+    got_a = lax.ppermute(cells_a, "tile", pairs_a)
+    return got_a, got_b
+
+
+def two_view_body(estimate, observed, psf_taps):
+    depth, rows, width = estimate.shape
+    own = width // LANES // 2
+    lanes = (own + 1) * LANES
+    near = rows // 2
+    view = lax.axis_index("view")
+    tile = lax.axis_index("tile")
+    last = lax.axis_size("tile") - 1
+    even = 1 - lax.rem(tile, 2)
+    swap = [(0, 1), (1, 0)]
+    meta = jnp.stack([view, even, tile == 0, tile == last]).astype(jnp.int32)
+    count = own * depth + depth // 2
+    count_mid = own * depth + depth // 4
+    window = shaped((2, depth, 2 * rows, lanes))
+
+    obs_own, est, theirs = call(
+        load_kernel,
+        [shaped(observed.shape), shaped(estimate.shape), shaped((count + 1, rows, LANES))],
+        [SMEM, HBM, HBM, VMEM],
+        scratch=[pltpu.SemaphoreType.DMA((depth,)), pltpu.SemaphoreType.DMA],
+    )(meta, in_hbm(observed), in_hbm(estimate), psf_taps)
+    other = lax.ppermute(theirs, "view", swap)
+    other_taps = other[count : count + 1, : psf_taps.shape[1], : psf_taps.shape[2]]
+    send = call(pack_kernel, shaped((count, rows, LANES)), [SMEM, VMEM])(meta, est)
+    got_a, got_b = paired(send, send)
+    own_a, own_b = paired(
+        *call(pack_near_kernel, [shaped((count, near, LANES))] * 2, [SMEM, VMEM])(meta, obs_own),
+    )
+
+    taps = jnp.concatenate([psf_taps, other_taps], axis=0)
+    normed = taps / jnp.sum(taps, axis=2, keepdims=True)
+    z_taps = normed[:, 0]
+    mats = call(
+        bands_kernel,
+        [
+            shaped((2, 2, rows, 6 * rows), BF),
+            shaped((2, 2, 3 * lanes, own * LANES), BF),
+            shaped((2, 2, 6 * LANES, LANES), BF),
+        ],
+        [SMEM, SMEM], scratch=[pltpu.VMEM((2, 3 * LANES, LANES), BF)],
+    )(meta, normed)
+    halo_a, halo_b = paired(
+        lax.dynamic_slice(other, (0, even * near, 0), (count, near, LANES)),
+        lax.dynamic_slice(other, (0, (1 - even) * near, 0), (count, near, LANES)),
+    )
+
+    stages = [
+        pltpu.VMEM((2, depth, 2 * rows, lanes), F32), pltpu.VMEM((2, depth, rows, lanes), F32),
+    ]
+    field = pltpu.VMEM((depth, 3 * rows, lanes), F32)
+    obs, ratio, gain = call(
+        first_kernel, [window, window, shaped((depth, rows, lanes))],
+        [SMEM, SMEM] + [VMEM] * 10, scratch=[field] + stages,
+    )(meta, z_taps, est, obs_own, got_a, got_b, own_a, own_b, other, *mats)
+    obs, _, current, cur_send = call(
+        update_kernel,
+        [window, window, shaped((depth, rows, lanes)), shaped((count_mid, rows, LANES))],
+        [SMEM, SMEM] + [VMEM] * 9, scratch=stages, input_output_aliases={4: 0, 5: 1},
+    )(meta, z_taps, est, gain, obs, ratio, halo_a, halo_b, *mats)
+    cur_a, cur_b = paired(cur_send, cur_send)
+    half = call(
+        second_kernel, shaped((depth, rows, own * LANES)),
+        [SMEM, SMEM] + [VMEM] * 7,
+        scratch=[field, pltpu.VMEM((2, depth, 2 * rows, lanes), F32)] + stages,
+    )(meta, z_taps, current, cur_a, cur_b, obs, *mats)
+    far = lax.ppermute(half, "view", swap)
+    partial = call(
+        place_kernel, shaped(estimate.shape), [SMEM, VMEM], HBM,
+        scratch=[pltpu.SemaphoreType.DMA((depth,))],
+    )(meta, half)
+    return lax.dynamic_update_slice(partial, far, (0, 0, (1 - view) * own * LANES))
 
 
 def extended_2(cells, sides, width):
@@ -68,7 +544,7 @@
     back_z = many_bands(flipped[:, 0], depth, depth, half)
     back_y = many_bands(flipped[:, 1], rows + 2 * half, rows, 0)
     fwd_y = many_bands(normed[:, 1], rows + 2 * half, rows, 0)
-    for step in range(ITERS):
+    for _ in range(ITERS):
         extended = extended_2(current, (("view", 2), ("tile", 1)), half)
         blurred = blur(extended, fwd_z, fwd_y, normed[:, 2], cols)
         ratio = recorded / blurred
@@ -80,8 +556,36 @@
     return current
 
 
+def fits(mesh, estimate, psf_taps):
+    depth, rows, width = estimate.shape
+    tiles = mesh.shape["tile"]
+    reach = (psf_taps.shape[2] - 1) // 2
+    return (
+        mesh.shape["view"] == 2
+        and tiles % 2 == 0
+        and rows % (32 * tiles) == 0
+        and rows // tiles >= 2 * (reach + 1)
+        and width % (2 * LANES) == 0
+        and 4 * reach <= LANES // 2
+        and 2 * reach <= LANES // 4
+        and depth % 4 == 0
+    )
+
+
 def solution(mesh):
     placed = (P(None, "tile", None), P("view", None, "tile", None), P("view", None, None))
-    return jax.shard_map(
-        body, mesh=mesh, in_specs=placed, out_specs=P(None, "tile", None), check_vma=False
-    )
+
+    def run(estimate, observed, psf_taps):
+        quick = fits(mesh, estimate, psf_taps)
+
+        def chosen(*blocks):
+            if not quick:
+                return body(*blocks)
+            return two_view_body(*blocks)
+
+        step = jax.shard_map(
+            chosen, mesh=mesh, in_specs=placed, out_specs=P(None, "tile", None), check_vma=False
+        )
+        return step(estimate, observed, psf_taps)
+
+    return run

time: 233 us -> 48.2 us (0.21)
  the two profiles are of different devices: /device:TPU:9 before, /device:TPU:18 now
where the time goes in v2:
time: 48.2 us; the launch traced here: 48 us
  Pallas kernels  16.4 us (34%)
  starting transfers between devices  15 us (31%)
  waiting for transfers between devices  14.8 us (31%)
  local copies, waits for them, and re-layouts  1.44 us (3%)
    ppermute x4, waiting for transfers between devices, paired(): got_b = lax.ppermute(cells_b, 'tile', pairs_b)  10.3 us
    ppermute x4, starting transfers between devices, paired(): got_b = lax.ppermute(cells_b, 'tile', pairs_b)  8.69 us
    pallas_call x1, Pallas kernels, two_view_body(): call(second_kernel, shaped((depth, rows, own * LANES)), [SMEM, SMEM] + [V...  4.52 us
    pallas_call x1, Pallas kernels, two_view_body(): call(first_kernel, [window, window, shaped((depth, rows, lanes))], [SMEM,...  3.84 us
    ppermute x1, waiting for transfers between devices, two_view_body(): far = lax.ppermute(half, 'view', swap)  3.71 us
    ppermute x4, starting transfers between devices, paired(): got_a = lax.ppermute(cells_a, 'tile', pairs_a)  3.32 us
    pallas_call x1, Pallas kernels, two_view_body(): call(load_kernel, [shaped(observed.shape), shaped(estimate.shape), shaped...  1.93 us
    pallas_call x1, Pallas kernels, two_view_body(): call(bands_kernel, [shaped((2, 2, rows, 6 * rows), BF), shaped((2, 2, 3 *...  1.89 us
  transfers between devices with their start and end apart: 10, of which 4 were waited for; matrix products, arithmetic and copies ran while one was open for 0% of the time, Pallas kernels for 17%

profile of v2, /device:TPU:18, one launch (start us, length us, event | category | flops | bytes accessed | tf_op | source)
XLA Modules:
  0.0 48.0 jit_solution(6237325979490804270)
XLA Ops:
  0.0 0.7 %copy.7.taps = f32[1,3,31]{2,1,0:T(4,128)S(1)} copy(f32[1,3,31]{2,0,1:T(1,128)} %param.5) | data formatting | bytes 744 | tf_op args[2]
  0.8 1.9 %shard_map.37 = (f32[1,8,32,512]{3,2,1,0:T(8,128)S(1)}, f32[8,32,512]{2,1,0:T(8,128)S(1)}, f32[21,32,128]{2,1,0:T(8,128)S(1)}) custom-call(s32[4]{0:T(128)S(1)} %pad_add_fusion.meta, f32[1,8,32,512]{3,2,1,0:T(8,128)} %obs_hbm.1, f32[8,32,512]{2,1,0:T(8,128)} %est_hbm.1, f32[1,3,31]{2,1,0:T(4,128)S(1)} %copy.7.taps), custom_call_target="tpu_custom_call" | custom-call | tf_op jit(solution)/shard_map/pallas_call | solution.py:427
  2.7 1.6 %collective-permute-start = (f32[21,32,128]{2,1,0:T(8,128)S(1)}, f32[21,32,128]{2,1,0:T(8,128)S(1)}, u32[]{:S(2)}, u32[]{:S(2)}) collective-permute-start(f32[21,32,128]{2,1,0:T(8,128)S(1)} %get-tuple-element.19), channel_id=1, source_target_pairs={{0,16},{16,0},{1,17},{17,1},{2,18},{18,2},{3,19},{19,3},{4,20},{20... | collective-permute-start | bytes 1032200 | tf_op jit(solution)/shard_map/ppermute | solution.py:433
  4.3 0.6 %shard_map.38 = f32[20,32,128]{2,1,0:T(8,128)S(1)} custom-call(s32[4]{0:T(128)S(1)} %pad_add_fusion.meta, f32[8,32,512]{2,1,0:T(8,128)S(1)} %get-tuple-element.20.est), custom_call_target="tpu_custom_call" | custom-call | tf_op jit(solution)/shard_map/pallas_call | solution.py:435
  4.9 1.9 %collective-permute-start.2 = (f32[20,32,128]{2,1,0:T(8,128)S(1)}, f32[20,32,128]{2,1,0:T(8,128)S(1)}, u32[]{:S(2)}, u32[]{:S(2)}) collective-permute-start(f32[20,32,128]{2,1,0:T(8,128)S(1)} %shard_map.38), channel_id=1, source_target_pairs={{1,2},{2,1},{3,4},{4,3},{5,6},{6,5},{7,8},{8,7},{9,10},{10,9},{11,... | collective-permute-start | bytes 983048 | tf_op jit(solution)/shard_map/ppermute | solution.py:407
  6.9 1.7 %collective-permute-start.1 = (f32[20,32,128]{2,1,0:T(8,128)S(1)}, f32[20,32,128]{2,1,0:T(8,128)S(1)}, u32[]{:S(2)}, u32[]{:S(2)}) collective-permute-start(f32[20,32,128]{2,1,0:T(8,128)S(1)} %shard_map.38), channel_id=1, source_target_pairs={{0,1},{1,0},{2,3},{3,2},{4,5},{5,4},{6,7},{7,6},{8,9},{9,8},{10,11... | collective-permute-start | bytes 983048 | tf_op jit(solution)/shard_map/ppermute | solution.py:408
  8.6 0.7 %shard_map.39 = (f32[20,16,128]{2,1,0:T(8,128)S(1)}, f32[20,16,128]{2,1,0:T(8,128)S(1)}) custom-call(s32[4]{0:T(128)S(1)} %pad_add_fusion.meta, f32[1,8,32,512]{3,2,1,0:T(8,128)S(1)} %get-tuple-element.21.obs.obs_own), custom_call_target="tpu_custom_call" | custom-call | tf_op jit(solution)/shard_map/pallas_call | solution.py:438
  9.3 0.1 collective-permute-start.3
  9.3 2.5 %collective-permute-start.4 = (f32[20,16,128]{2,1,0:T(8,128)S(1)}, f32[20,16,128]{2,1,0:T(8,128)S(1)}, u32[]{:S(2)}, u32[]{:S(2)}) collective-permute-start(f32[20,16,128]{2,1,0:T(8,128)S(1)} %get-tuple-element.23), channel_id=1, source_target_pairs={{1,2},{2,1},{3,4},{4,3},{5,6},{6,5},{7,8},{8,7},{9,10},{10,9},{11,... | collective-permute-start | bytes 491528 | tf_op jit(solution)/shard_map/ppermute | solution.py:407
  11.8 0.7 %collective-permute-done.other = f32[21,32,128]{2,1,0:T(8,128)S(1)} collective-permute-done((f32[21,32,128]{2,1,0:T(8,128)S(1)}, f32[21,32,128]{2,1,0:T(8,128)S(1)}, u32[]{:S(2)}, u32[]{:S(2)}) %collective-permute-start) | collective-permute-done | bytes 344096 | tf_op jit(solution)/shard_map/ppermute | solution.py:433
  12.6 2.4 %collective-permute-start.6 = (f32[20,16,128]{2,1,0:T(8,128)S(1)}, f32[20,16,128]{2,1,0:T(8,128)S(1)}, u32[]{:S(2)}, u32[]{:S(2)}) collective-permute-start(f32[20,16,128]{2,1,0:T(8,128)S(1)} %get-tuple-element.33), channel_id=1, source_target_pairs={{1,2},{2,1},{3,4},{4,3},{5,6},{6,5},{7,8},{8,7},{9,10},{10,9},{11,... | collective-permute-start | bytes 491528 | tf_op jit(solution)/shard_map/ppermute | solution.py:407
  15.0 1.4 %collective-permute-start.5 = (f32[20,16,128]{2,1,0:T(8,128)S(1)}, f32[20,16,128]{2,1,0:T(8,128)S(1)}, u32[]{:S(2)}, u32[]{:S(2)}) collective-permute-start(f32[20,16,128]{2,1,0:T(8,128)S(1)} %get-tuple-element.34), channel_id=1, source_target_pairs={{0,1},{1,0},{2,3},{3,2},{4,5},{5,4},{6,7},{7,6},{8,9},{9,8},{10,11... | collective-permute-start | bytes 491528 | tf_op jit(solution)/shard_map/ppermute | solution.py:408
  16.4 0.1 fusion.taps
  16.5 1.9 %shard_map.40 = (bf16[2,2,32,192]{3,2,1,0:T(8,128)(2,1)S(1)}, bf16[2,2,1152,256]{3,2,1,0:T(8,128)(2,1)S(1)}, bf16[2,2,768,128]{3,2,1,0:T(8,128)(2,1)S(1)}) custom-call(s32[4]{0:T(128)S(1)} %pad_add_fusion.meta, f32[2,3,31]{2,1,0:T(4,128)S(1)} %fusion.taps), custom_call_target="tpu_custom_call" | custom-call | tf_op jit(solution)/shard_map/pallas_call | solution.py:444
  18.4 3.7 %collective-permute-done.4.own_b = f32[20,16,128]{2,1,0:T(8,128)S(1)} collective-permute-done((f32[20,16,128]{2,1,0:T(8,128)S(1)}, f32[20,16,128]{2,1,0:T(8,128)S(1)}, u32[]{:S(2)}, u32[]{:S(2)}) %collective-permute-start.4) | collective-permute-done | bytes 163872 | tf_op jit(solution)/shard_map/ppermute | solution.py:407
  22.1 3.8 %shard_map.41 = (f32[2,8,64,384]{3,2,1,0:T(8,128)S(1)}, f32[2,8,64,384]{3,2,1,0:T(8,128)S(1)}, f32[8,32,384]{2,1,0:T(8,128)S(1)}) custom-call(s32[4]{0:T(128)S(1)} %pad_add_fusion.meta, f32[2,31]{1,0:T(2,128)S(1)} %bitcast.5, f32[8,32,512]{2,1,0:T(8,128)S(1)} %get-tuple-element.20.est, f32[1,8,32,512]{3,2,1,0:T(8,128)S(1)} %get-tuple-element.21.obs.obs_own, ...), custom_call_target="tpu_custom_call" | custom-call | tf_op jit(solution)/shard_map/pallas_call | solution.py:462
  26.0 1.6 %shard_map.42 = (f32[2,8,64,384]{3,2,1,0:T(8,128)S(1)}, f32[2,8,64,384]{3,2,1,0:T(8,128)S(1)}, f32[8,32,384]{2,1,0:T(8,128)S(1)}, f32[18,32,128]{2,1,0:T(8,128)S(1)}) custom-call(s32[4]{0:T(128)S(1)} %pad_add_fusion.meta, f32[2,31]{1,0:T(2,128)S(1)} %bitcast.6, ...), custom_call_target="tpu_custom_call", output_to_operand_aliasing={{0}: (4, {}), {1}: (5, {})} | custom-call | tf_op jit(solution)/shard_map/pallas_call | solution.py:466
  27.6 1.9 %collective-permute-start.8 = (f32[18,32,128]{2,1,0:T(8,128)S(1)}, f32[18,32,128]{2,1,0:T(8,128)S(1)}, u32[]{:S(2)}, u32[]{:S(2)}) collective-permute-start(f32[18,32,128]{2,1,0:T(8,128)S(1)} %get-tuple-element.31), channel_id=1, source_target_pairs={{1,2},{2,1},{3,4},{4,3},{5,6},{6,5},{7,8},{8,7},{9,10},{10,9},{11,... | collective-permute-start | bytes 884744 | tf_op jit(solution)/shard_map/ppermute | solution.py:407
  29.6 6.6 %collective-permute-done.8.got_b = f32[18,32,128]{2,1,0:T(8,128)S(1)} collective-permute-done((f32[18,32,128]{2,1,0:T(8,128)S(1)}, f32[18,32,128]{2,1,0:T(8,128)S(1)}, u32[]{:S(2)}, u32[]{:S(2)}) %collective-permute-start.8) | collective-permute-done | bytes 294944 | tf_op jit(solution)/shard_map/ppermute | solution.py:407
  36.3 4.5 %shard_map.43.half = f32[8,32,256]{2,1,0:T(8,128)S(1)} custom-call(s32[4]{0:T(128)S(1)} %pad_add_fusion.meta, f32[2,31]{1,0:T(2,128)S(1)} %bitcast.7, f32[8,32,384]{2,1,0:T(8,128)S(1)} %get-tuple-element.30.current, f32[18,32,128]{2,1,0:T(8,128)S(1)} %collective-permute-done.7.got_a, f32[18,32,128]{2,1,0:T(8,128)S(1)} %collective-permute-done.8.got_b, ...), custom_call_target="tpu_custom_call" | custom-call | tf_op jit(solution)/shard_map/pallas_call | solution.py:472
  40.8 1.4 %collective-permute-start.9 = (f32[8,32,256]{2,1,0:T(8,128)S(1)}, f32[8,32,256]{2,1,0:T(8,128)S(1)}, u32[]{:S(2)}, u32[]{:S(2)}) collective-permute-start(f32[8,32,256]{2,1,0:T(8,128)S(1)} %shard_map.43.half), channel_id=1, source_target_pairs={{0,16},{16,0},{1,17},{17,1},{2,18},{18,2},{3,19},{19,3},{4,20},{20... | collective-permute-start | bytes 786440 | tf_op jit(solution)/shard_map/ppermute | solution.py:477
  42.2 1.3 %shard_map.44 = f32[8,32,512]{2,1,0:T(8,128)} custom-call(s32[4]{0:T(128)S(1)} %pad_add_fusion.meta, f32[8,32,256]{2,1,0:T(8,128)S(1)} %shard_map.43.half), custom_call_target="tpu_custom_call" | custom-call | tf_op jit(solution)/shard_map/pallas_call | solution.py:478
  43.5 3.7 %collective-permute-done.9 = f32[8,32,256]{2,1,0:T(8,128)S(1)} collective-permute-done((f32[8,32,256]{2,1,0:T(8,128)S(1)}, f32[8,32,256]{2,1,0:T(8,128)S(1)}, u32[]{:S(2)}, u32[]{:S(2)}) %collective-permute-start.9) | collective-permute-done | bytes 262176 | tf_op jit(solution)/shard_map/ppermute | solution.py:477
  47.2 0.7 %constant_dynamic-update-slice_fusion = f32[8,32,512]{2,1,0:T(8,128)} fusion(f32[8,32,512]{2,1,0:T(8,128)} %shard_map.44, f32[8,32,256]{2,1,0:T(8,128)S(1)} %collective-permute-done.9, s32[]{:T(128)S(6)} %select_n.11), kind=kLoop, calls=%fused_computation.3 | loop fusion | bytes 524292 | tf_op jit(solution)/shard_map/dynamic_update_slice | solution.py:482
  (11 shorter events, 0.2 us)
Async XLA Ops:
  2.7 9.9 %collective-permute-start = (f32[21,32,128]{2,1,0:T(8,128)S(1)}, f32[21,32,128]{2,1,0:T(8,128)S(1)}, u32[]{:S(2)}, u32[]{:S(2)}) collective-permute-start(f32[21,32,128]{2,1,0:T(8,128)S(1)} %get-tuple-element.19), channel_id=1, source_target_pairs={{0,16},{16,0},{1,17},{17,1},{2,18},{18,2},{3,19},{19,3},{4,20},{20... | collective-permute-start | bytes 1032200 | tf_op jit(solution)/shard_map/ppermute | solution.py:433
  4.9 17.2 %collective-permute-start.2 = (f32[20,32,128]{2,1,0:T(8,128)S(1)}, f32[20,32,128]{2,1,0:T(8,128)S(1)}, u32[]{:S(2)}, u32[]{:S(2)}) collective-permute-start(f32[20,32,128]{2,1,0:T(8,128)S(1)} %shard_map.38), channel_id=1, source_target_pairs={{1,2},{2,1},{3,4},{4,3},{5,6},{6,5},{7,8},{8,7},{9,10},{10,9},{11,... | collective-permute-start | bytes 983048 | tf_op jit(solution)/shard_map/ppermute | solution.py:407
  6.9 15.2 %collective-permute-start.1 = (f32[20,32,128]{2,1,0:T(8,128)S(1)}, f32[20,32,128]{2,1,0:T(8,128)S(1)}, u32[]{:S(2)}, u32[]{:S(2)}) collective-permute-start(f32[20,32,128]{2,1,0:T(8,128)S(1)} %shard_map.38), channel_id=1, source_target_pairs={{0,1},{1,0},{2,3},{3,2},{4,5},{5,4},{6,7},{7,6},{8,9},{9,8},{10,11... | collective-permute-start | bytes 983048 | tf_op jit(solution)/shard_map/ppermute | solution.py:408
  9.3 5.7 %collective-permute-start.3 = (f32[20,16,128]{2,1,0:T(8,128)S(1)}, f32[20,16,128]{2,1,0:T(8,128)S(1)}, u32[]{:S(2)}, u32[]{:S(2)}) collective-permute-start(f32[20,16,128]{2,1,0:T(8,128)S(1)} %get-tuple-element.22), channel_id=1, source_target_pairs={{0,1},{1,0},{2,3},{3,2},{4,5},{5,4},{6,7},{7,6},{8,9},{9,8},{10,11... | collective-permute-start | bytes 491528 | tf_op jit(solution)/shard_map/ppermute | solution.py:408
  9.3 12.8 %collective-permute-start.4 = (f32[20,16,128]{2,1,0:T(8,128)S(1)}, f32[20,16,128]{2,1,0:T(8,128)S(1)}, u32[]{:S(2)}, u32[]{:S(2)}) collective-permute-start(f32[20,16,128]{2,1,0:T(8,128)S(1)} %get-tuple-element.23), channel_id=1, source_target_pairs={{1,2},{2,1},{3,4},{4,3},{5,6},{6,5},{7,8},{8,7},{9,10},{10,9},{11,... | collective-permute-start | bytes 491528 | tf_op jit(solution)/shard_map/ppermute | solution.py:407
  12.6 13.4 %collective-permute-start.6 = (f32[20,16,128]{2,1,0:T(8,128)S(1)}, f32[20,16,128]{2,1,0:T(8,128)S(1)}, u32[]{:S(2)}, u32[]{:S(2)}) collective-permute-start(f32[20,16,128]{2,1,0:T(8,128)S(1)} %get-tuple-element.33), channel_id=1, source_target_pairs={{1,2},{2,1},{3,4},{4,3},{5,6},{6,5},{7,8},{8,7},{9,10},{10,9},{11,... | collective-permute-start | bytes 491528 | tf_op jit(solution)/shard_map/ppermute | solution.py:407
  15.0 11.0 %collective-permute-start.5 = (f32[20,16,128]{2,1,0:T(8,128)S(1)}, f32[20,16,128]{2,1,0:T(8,128)S(1)}, u32[]{:S(2)}, u32[]{:S(2)}) collective-permute-start(f32[20,16,128]{2,1,0:T(8,128)S(1)} %get-tuple-element.34), channel_id=1, source_target_pairs={{0,1},{1,0},{2,3},{3,2},{4,5},{5,4},{6,7},{7,6},{8,9},{9,8},{10,11... | collective-permute-start | bytes 491528 | tf_op jit(solution)/shard_map/ppermute | solution.py:408
  27.6 8.7 %collective-permute-start.8 = (f32[18,32,128]{2,1,0:T(8,128)S(1)}, f32[18,32,128]{2,1,0:T(8,128)S(1)}, u32[]{:S(2)}, u32[]{:S(2)}) collective-permute-start(f32[18,32,128]{2,1,0:T(8,128)S(1)} %get-tuple-element.31), channel_id=1, source_target_pairs={{1,2},{2,1},{3,4},{4,3},{5,6},{6,5},{7,8},{8,7},{9,10},{10,9},{11,... | collective-permute-start | bytes 884744 | tf_op jit(solution)/shard_map/ppermute | solution.py:407
  29.5 6.7 %collective-permute-start.7 = (f32[18,32,128]{2,1,0:T(8,128)S(1)}, f32[18,32,128]{2,1,0:T(8,128)S(1)}, u32[]{:S(2)}, u32[]{:S(2)}) collective-permute-start(f32[18,32,128]{2,1,0:T(8,128)S(1)} %get-tuple-element.31), channel_id=1, source_target_pairs={{0,1},{1,0},{2,3},{3,2},{4,5},{5,4},{6,7},{7,6},{8,9},{9,8},{10,11... | collective-permute-start | bytes 884744 | tf_op jit(solution)/shard_map/ppermute | solution.py:408
  40.8 6.4 %collective-permute-start.9 = (f32[8,32,256]{2,1,0:T(8,128)S(1)}, f32[8,32,256]{2,1,0:T(8,128)S(1)}, u32[]{:S(2)}, u32[]{:S(2)}) collective-permute-start(f32[8,32,256]{2,1,0:T(8,128)S(1)} %shard_map.43.half), channel_id=1, source_target_pairs={{0,16},{16,0},{1,17},{17,1},{2,18},{18,2},{3,19},{19,3},{4,20},{20... | collective-permute-start | bytes 786440 | tf_op jit(solution)/shard_map/ppermute | solution.py:477

commit v3 on v2

v3 whole, which is shorter than its diff:
```python
import jax
import jax.numpy as jnp
from jax import lax
from jax.experimental import pallas as pl
from jax.experimental.pallas import tpu as pltpu
from jax.sharding import PartitionSpec as P


ITERS = 2
LANES = 128
VMEM_BYTES = 24 << 20
BF = jnp.bfloat16
F32 = jnp.float32
VMEM = pl.BlockSpec(memory_space=pltpu.VMEM)
SMEM = pl.BlockSpec(memory_space=pltpu.SMEM)
HBM = pl.BlockSpec(memory_space=pltpu.HBM)


def shaped(shape, dtype=F32):
    return jax.ShapeDtypeStruct(shape, dtype)


def call(kernel, outs, in_specs, out_specs=None, scratch=(), **more):
    return pl.pallas_call(
        kernel, out_shape=outs, in_specs=in_specs,
        out_specs=out_specs or jax.tree.map(lambda _: VMEM, outs), scratch_shapes=scratch,
        compiler_params=pltpu.CompilerParams(vmem_limit_bytes=VMEM_BYTES), **more,
    )


def in_hbm(cells):
    return pltpu.with_memory_space_constraint(cells, pltpu.HBM)


def split(cells):
    high = cells.astype(BF)
    return high, (cells - high.astype(F32)).astype(BF)


def block_at(view, place, blocks):
    at = jnp.where(view == 0, place, blocks - 1 - place)
    return pl.ds(pl.multiple_of(at * LANES, LANES), LANES)


def fold(planes, view, parts):
    piece = LANES // parts
    lane = lax.broadcasted_iota(jnp.int32, planes[0].shape, 1)
    first = jnp.where(view == 0, 0, piece)
    total = None
    for at, plane in enumerate(planes):
        moved = pltpu.roll(plane, lax.rem(first + at * piece, LANES), 1)
        total = moved if total is None else jnp.where(lane >= at * piece, moved, total)
    return total


def unfold(folded, view, parts, at):
    piece = LANES // parts
    first = jnp.where(view == 0, LANES, LANES - piece)
    return pltpu.roll(folded, lax.rem(first - at * piece, LANES), 1)


def pack_window(view, planes_of, depth, own, parts, out_ref):
    for place in range(own):
        for z in range(depth):
            out_ref[place * depth + z] = planes_of(z, place)
    for group in range(depth // parts):
        planes = [planes_of(group * parts + at, own) for at in range(parts)]
        out_ref[own * depth + group] = fold(planes, view, parts)


def unpack_window(view, packed_of, depth, own, parts, store):
    for place in range(own):
        for z in range(depth):
            store(z, place, packed_of(place * depth + z))
    for group in range(depth // parts):
        folded = packed_of(own * depth + group)
        for at in range(parts):
            store(group * parts + at, own, unfold(folded, view, parts, at))


def plane_copies(cells_hbm, cells, sems):
    copies = [
        pltpu.make_async_copy(cells_hbm.at[z], cells.at[z], sems.at[z])
        for z in range(cells.shape[0])
    ]
    for copy in copies:
        copy.start()
    return copies


def pack_pair(view, plane_of, z, depth, own, out):
    for at in (z, z + 1):
        for place in range(own):
            out[place * depth + at] = plane_of(at, place)
    out[own * depth + z // 2] = fold([plane_of(at, own) for at in (z, z + 1)], view, 2)


def near_rows(even, rows):
    near = rows // 2
    at_a = pl.multiple_of(jnp.where(even == 1, near, 0), near)
    at_b = pl.multiple_of(jnp.where(even == 1, 0, near), near)
    return at_a, at_b


def load_kernel(
    meta, est_hbm, obs_hbm, taps_hbm, est, obs, taps, send, theirs_a, theirs_b, near_a, near_b,
    est_sems, obs_sems, taps_sem
):
    depth, rows, width = est.shape
    blocks = width // LANES
    own = blocks // 2
    near = rows // 2
    view = meta[0]
    est_copies = plane_copies(est_hbm, est, est_sems)
    obs_copies = plane_copies(obs_hbm.at[0], obs.at[0], obs_sems)
    taps_copy = pltpu.make_async_copy(taps_hbm, taps, taps_sem)
    taps_copy.start()
    for z in range(0, depth, 2):
        est_copies[z].wait()
        est_copies[z + 1].wait()
        pack_pair(view, lambda at, p: est[at, :, block_at(view, p, blocks)], z, depth, own, send)
    for z in range(0, depth, 2):
        obs_copies[z].wait()
        obs_copies[z + 1].wait()
        for window, outs in ((1 - view, (theirs_a, theirs_b)), (view, (near_a, near_b))):
            for out, start in zip(outs, near_rows(meta[1], rows)):
                pack_pair(
                    window,
                    lambda at, p, window=window, start=start: obs[
                        0, at, pl.ds(start, near), block_at(window, p, blocks)
                    ],
                    z, depth, own, out,
                )
    taps_copy.wait()


def bands_kernel(meta, taps, y_out, own_mats, ext_mats, band):
    length = taps.shape[2]
    reach = (length - 1) // 2
    rows = y_out.shape[2]
    span = 2 * rows
    low = (LANES - reach) // 16 * 16
    high = -(-(2 * LANES + reach) // 16) * 16
    at_before = pl.multiple_of(jnp.where(meta[0] == 0, low, 2 * LANES + low), 16)
    at_after = pl.multiple_of(jnp.where(meta[0] == 0, 2 * LANES, 0), 16)
    lag = (
        lax.broadcasted_iota(jnp.int32, (high - low, LANES), 0)
        + (low - LANES)
        - lax.broadcasted_iota(jnp.int32, (high - low, LANES), 1)
    )
    r_at = lax.broadcasted_iota(jnp.int32, (rows, 3 * span), 0)
    s_at = lax.broadcasted_iota(jnp.int32, (rows, 3 * span), 1)
    y_lag = lax.rem(s_at, span) - r_at - rows // 2
    band[...] = jnp.zeros_like(band)
    kinds = [(view, back) for view in range(2) for back in range(2)]

    def banded(lag, axis):
        bands = [jnp.zeros(lag.shape, F32)] * 4
        for at in range(-reach, reach + 1):
            here = lag == at
            for n, (view, back) in enumerate(kinds):
                tap = taps[axis, view, reach - at if back else reach + at]
                bands[n] = jnp.where(here, tap, bands[n])
        return bands

    piece = 16
    for start in range(0, high - low, piece):
        row = low + start
        for n, cells in enumerate(banded(lag[start : start + piece], 2)):
            for which, part in enumerate(split(cells)):
                if row < LANES:
                    band[n, which, pl.ds(at_before + start, piece)] = part
                elif row < 2 * LANES:
                    band[n, which, row : row + piece] = part
                else:
                    band[n, which, pl.ds(at_after + (row - 2 * LANES), piece)] = part
    for n, (view, back) in enumerate(kinds):
        spread_x(band.at[n], own_mats.at[view, back], ext_mats.at[view, back])
    for start in range(0, rows, piece):
        at = slice(start, start + piece)
        for n, y_band in enumerate(banded(y_lag[at], 1)):
            y_high = y_band.astype(BF).astype(F32)
            y_out[kinds[n][0], kinds[n][1], at] = jnp.where(
                s_at[at] < 2 * span, y_high, y_band - y_high
            ).astype(BF)


def spread_x(band, own_mat, ext_mat):
    own = own_mat.shape[1] // LANES
    for part, which in enumerate((0, 1, 0)):
        for src in range(own + 1):
            at = (part * (own + 1) + src) * LANES
            for dst in range(own):
                if abs(src - dst) <= 1:
                    start = (src - dst + 1) * LANES
                    cells = band[which, start : start + LANES, :]
                else:
                    cells = jnp.zeros((LANES, LANES), BF)
                own_mat[at : at + LANES, dst * LANES : (dst + 1) * LANES] = cells
        for src in range(2):
            at = (part * 2 + src) * LANES
            ext_mat[at : at + LANES, :] = band[which, src * LANES : (src + 1) * LANES, :]


def y_stage(source, bands):
    high, low = split(source)
    return jnp.dot(bands, jnp.concatenate([high, low, high], axis=0), preferred_element_type=F32)


def z_stage(taps, view, back, inner, base, rows, outer):
    depth = inner.shape[0]
    reach = (taps.shape[1] - 1) // 2
    for row in range(0, rows, 8):
        planes = [inner[z, base + row : base + row + 8, :] for z in range(depth)]
        for out in range(depth):
            total = None
            for z in range(depth):
                at = reach + (out - z if back else z - out)
                term = taps[view, at] * planes[z]
                total = term if total is None else total + term
            outer[out, row : row + 8, :] = total


def x_stage(cells, own_mat, ext_mat):
    lead, lanes = cells.shape[:-1], cells.shape[-1]
    high, low = split(cells.reshape(-1, lanes))
    left = jnp.concatenate([high, high, low], axis=1)
    own = jnp.dot(left, own_mat[...], preferred_element_type=F32).reshape(*lead, -1)
    if ext_mat is None:
        return own, None
    at = lanes - 2 * LANES
    left = jnp.concatenate([high[:, at:], high[:, at:], low[:, at:]], axis=1)
    ext = jnp.dot(left, ext_mat[...], preferred_element_type=F32).reshape(*lead, LANES)
    return own, ext


def forward_half(source, half, z_taps, y_bands, own_mats, ext_mats, inner, outer, emit):
    depth = inner.shape[1]
    rows = outer.shape[2]
    both = jnp.concatenate([y_bands[0, 0], y_bands[1, 0]], axis=0)
    for z in range(depth):
        inner[half, z] = y_stage(source(z), both)
    for view in range(2):
        z_stage(z_taps, view, False, inner.at[half], view * rows, rows, outer.at[view])
        emit(view, *x_stage(outer[view], own_mats.at[view, 0], ext_mats.at[view, 0]))


def backward(ratio, view, z_taps, y_bands, own_mats, ext_mats, inner, outer):
    depth = ratio.shape[0]
    rows = outer.shape[2]
    for z in range(depth):
        inner[view, z, :rows, :] = y_stage(ratio[z], y_bands[view, 1])
    z_stage(z_taps, view, True, inner.at[view], 0, rows, outer.at[view])
    ext_mat = None if ext_mats is None else ext_mats.at[view, 1]
    return x_stage(outer[view], own_mats.at[view, 1], ext_mat)


def halo_rows(even, rows):
    near = rows // 2
    at_a = pl.multiple_of(jnp.where(even == 1, rows + near, 0), near)
    at_b = pl.multiple_of(jnp.where(even == 1, 0, rows + near), near)
    return at_a, at_b


def cols(place):
    return slice(place * LANES, (place + 1) * LANES)


def half_forward(meta, below, z_taps, got, parts, mats, field, inner, outer, emit):
    depth, rows = field.shape[0], field.shape[1] // 2
    own = field.shape[2] // LANES - 1
    got_at = pl.multiple_of(jnp.where(below, rows, 0), rows)

    def store(z, place, cells):
        field[z, pl.ds(got_at, rows), cols(place)] = cells

    unpack_window(meta[0], lambda n: got[n], depth, own, parts, store)

    def emit_at(v, own_cells, ext):
        for place in range(own + 1):
            cells = ext if place == own else own_cells[:, :, cols(place)]
            emit(v, got_at, place, cells)

    forward_half(lambda z: field[z], 0, z_taps, *mats, inner, outer, emit_at)


def own_rows(below, rows):
    return pl.ds(pl.multiple_of(jnp.where(below, 0, rows), rows), rows)


def first_kernel(
    meta, z_taps, est, obs_own, got_a, got_b, other_a, other_b, y_bands, own_mats, ext_mats,
    obs, ratio, field, inner, outer
):
    depth, rows, width = est.shape
    own = width // LANES // 2
    view = meta[0]
    near = rows // 2
    for place in range(own + 1):
        field[:, rows : 2 * rows, cols(place)] = est[:, :, block_at(view, place, width // LANES)]
        obs[0, :, near : near + rows, cols(place)] = obs_own[
            0, :, :, block_at(view, place, width // LANES)
        ]
    for other, start in zip((other_a, other_b), near_rows(meta[1], rows)):
        at = pl.ds(pl.multiple_of(start + near, near), near)

        def store_other(z, place, cells, at=at):
            obs[1, z, at, cols(place)] = cells

        unpack_window(view, lambda n, other=other: other[n], depth, own, 2, store_other)
    at_a = pl.multiple_of(jnp.where(meta[1] == 1, 2 * rows, 0), rows)
    at_b = pl.multiple_of(jnp.where(meta[1] == 1, 0, 2 * rows), rows)
    for got, at in ((got_a, at_a), (got_b, at_b)):

        def store(z, place, cells, at=at):
            field[z, pl.ds(at, rows), cols(place)] = cells

        unpack_window(view, lambda n, got=got: got[n], depth, own, 2, store)
    both = jnp.concatenate([y_bands[0, 0], y_bands[1, 0]], axis=0)
    for half in range(2):
        for z in range(depth):
            inner[half, z] = y_stage(field[z, half * rows : half * rows + 2 * rows, :], both)
    for v in range(2):
        for half in range(2):
            z_stage(z_taps, v, False, inner.at[half], v * rows, rows, outer.at[v, half])
        own_cells, ext = x_stage(outer[v], own_mats.at[v, 0], ext_mats.at[v, 0])
        for half in range(2):
            for place in range(own + 1):
                cells = ext[half] if place == own else own_cells[half][:, :, cols(place)]
                for quarter in range(2):
                    part = cells[:, quarter * near : (quarter + 1) * near]
                    at = half * rows + quarter * near
                    at = slice(at, at + near)
                    if half != quarter:
                        part = obs[v, :, at, cols(place)] / part
                    ratio[v, :, at, cols(place)] = part


def complete(meta, which, halo_a, halo_b, obs, ratio_in, ratio):
    depth, rows, lanes = obs.shape[1], obs.shape[2] // 2, obs.shape[3]
    near = rows // 2
    own = lanes // LANES - 1
    for halo, at in zip((halo_a, halo_b), halo_rows(meta[1], rows)):
        known = jnp.where(at == 0, 1 - meta[2], 1 - meta[3]) == 1

        def store(z, place, cells, at=at, known=known):
            obs[which, z, pl.ds(at, near), cols(place)] = cells
            blurred = ratio_in[which, z, pl.ds(at, near), cols(place)]
            ratio[which, z, pl.ds(at, near), cols(place)] = jnp.where(known, cells / blurred, 0.0)

        unpack_window(meta[0], lambda n, halo=halo: halo[n], depth, own, 2, store)


def update_kernel(
    meta, z_taps, est, obs_in, ratio_in, own_a, own_b, far_a, far_b, y_bands, own_mats, ext_mats,
    obs, ratio, current, to_send, inner, outer
):
    depth, _, width = est.shape
    own = width // LANES // 2
    view = meta[0]
    backs = []
    for v, halos in enumerate(((own_a, own_b), (far_a, far_b))):
        complete(meta, v, *halos, obs, ratio_in, ratio)
        backs.append(backward(ratio.at[v], v, z_taps, y_bands, own_mats, ext_mats, inner, outer))
    for place in range(own + 1):
        cells = est[:, :, block_at(view, place, width // LANES)]
        mine, other = [
            back[1] if place == own else back[0][:, :, cols(place)] for back in backs
        ]
        current[:, :, cols(place)] = cells * jnp.sqrt(mine * other)
    pack_window(view, lambda z, p: current[z, :, cols(p)], depth, own, 4, to_send)


def second_half(meta, below, z_taps, current, got, obs, mats, ratio, field, inner, outer):
    rows = current.shape[1]
    field[:, own_rows(below, rows), :] = current[...]
    low = jnp.where(meta[2] == 1, rows // 2, 0)
    high = jnp.where(meta[3] == 1, rows + rows // 2, 2 * rows)
    row = lax.broadcasted_iota(jnp.int32, (rows, LANES), 0)

    def emit(v, at, place, cells):
        inside = ((row + at >= low) & (row + at < high))[None]
        where = (v, slice(None), pl.ds(at, rows), cols(place))
        ratio[where] = jnp.where(inside, obs[where] / cells, 0.0)

    half_forward(meta, below, z_taps, got, 4, mats, field, inner, outer, emit)


def second_a_kernel(
    meta, z_taps, current, got_a, obs, y_bands, own_mats, ext_mats,
    ratio, field, inner, outer
):
    mats = (y_bands, own_mats, ext_mats)
    second_half(
        meta, meta[1] == 1, z_taps, current, got_a, obs, mats, ratio, field, inner, outer
    )


def second_b_kernel(
    meta, z_taps, current, got_b, obs, ratio_in, y_bands, own_mats, ext_mats,
    out, ratio, field, inner, outer
):
    own = current.shape[2] // LANES - 1
    mats = (y_bands, own_mats, ext_mats)
    second_half(
        meta, meta[1] != 1, z_taps, current, got_b, obs, mats, ratio, field, inner, outer
    )
    gains = [
        backward(ratio.at[v], v, z_taps, y_bands, own_mats, None, inner, outer)[0]
        for v in range(2)
    ]
    result = current[:, :, : own * LANES] * jnp.sqrt(gains[0] * gains[1])
    for place in range(own):
        at = jnp.where(meta[0] == 0, place, own - 1 - place)
        out[:, :, pl.ds(pl.multiple_of(at * LANES, LANES), LANES)] = result[:, :, cols(place)]


def copy_planes(cells, out, at, sems):
    width = cells.shape[2]
    copies = [
        pltpu.make_async_copy(cells.at[z], out.at[z, :, pl.ds(at, width)], sems.at[z])
        for z in range(cells.shape[0])
    ]
    for copy in copies:
        copy.start()
    for copy in copies:
        copy.wait()


def place_kernel(meta, half, out, sems):
    width = half.shape[2]
    copy_planes(half, out, pl.multiple_of(meta[0] * width, width), sems)


def paired(cells_a, cells_b):
    count = lax.axis_size("tile")
    pairs_a = [(i, i ^ 1) for i in range(count)]
    pairs_b = []
    for i in range(1, count - 1, 2):
        pairs_b += [(i, i + 1), (i + 1, i)]
    got_b = lax.ppermute(cells_b, "tile", pairs_b)
    got_a = lax.ppermute(cells_a, "tile", pairs_a)
    return got_a, got_b


def two_view_body(estimate, observed, psf_taps):
    depth, rows, width = estimate.shape
    own = width // LANES // 2
    lanes = (own + 1) * LANES
    near = rows // 2
    view = lax.axis_index("view")
    tile = lax.axis_index("tile")
    last = lax.axis_size("tile") - 1
    even = 1 - lax.rem(tile, 2)
    swap = [(0, 1), (1, 0)]
    meta = jnp.stack([view, even, tile == 0, tile == last]).astype(jnp.int32)
    count = own * depth + depth // 2
    count_mid = own * depth + depth // 4
    window = shaped((2, depth, 2 * rows, lanes))

    kinds = jnp.transpose(psf_taps, (1, 0, 2))
    packed = shaped((count, rows, LANES))
    packed_near = shaped((count, near, LANES))
    est, obs_own, own_taps, send, theirs_a, theirs_b, near_a, near_b = call(
        load_kernel,
        [shaped(cells.shape) for cells in (estimate, observed, kinds)]
        + [packed] + [packed_near] * 4,
        [SMEM, HBM, HBM, HBM],
        scratch=[pltpu.SemaphoreType.DMA((depth,))] * 2 + [pltpu.SemaphoreType.DMA],
    )(meta, in_hbm(estimate), in_hbm(observed), in_hbm(kinds))
    got_a, got_b = paired(send, send)
    other_b = lax.ppermute(theirs_b, "view", swap)
    other_a = lax.ppermute(theirs_a, "view", swap)
    other_taps = lax.ppermute(own_taps, "view", swap)
    own_a, own_b = paired(near_a, near_b)

    taps = jnp.concatenate([own_taps, other_taps], axis=1)
    normed = taps / jnp.sum(taps, axis=2, keepdims=True)
    z_taps = normed[0]
    mats = call(
        bands_kernel,
        [
            shaped((2, 2, rows, 6 * rows), BF),
            shaped((2, 2, 3 * lanes, own * LANES), BF),
            shaped((2, 2, 6 * LANES, LANES), BF),
        ],
        [SMEM, SMEM], scratch=[pltpu.VMEM((4, 2, 3 * LANES, LANES), BF)],
    )(meta, normed)
    halo_a, halo_b = paired(other_a, other_b)

    stages = [
        pltpu.VMEM((2, depth, 2 * rows, lanes), F32), pltpu.VMEM((2, depth, rows, lanes), F32),
    ]
    scratch = [pltpu.VMEM((depth, 2 * rows, lanes), F32)] + stages
    obs, ratio = call(
        first_kernel, [window, window], [SMEM, SMEM] + [VMEM] * 9,
        scratch=[
            pltpu.VMEM((depth, 3 * rows, lanes), F32), stages[0],
            pltpu.VMEM((2, 2, depth, rows, lanes), F32),
        ],
    )(meta, z_taps, est, obs_own, got_a, got_b, other_a, other_b, *mats)
    obs, _, current, cur_send = call(
        update_kernel,
        [window, window, shaped((depth, rows, lanes)), shaped((count_mid, rows, LANES))],
        [SMEM, SMEM] + [VMEM] * 10, scratch=stages, input_output_aliases={3: 0, 4: 1},
    )(meta, z_taps, est, obs, ratio, own_a, own_b, halo_a, halo_b, *mats)
    cur_a, cur_b = paired(cur_send, cur_send)
    ratio = call(
        second_a_kernel, window, [SMEM, SMEM] + [VMEM] * 6, scratch=scratch
    )(meta, z_taps, current, cur_a, obs, *mats)
    half, _ = call(
        second_b_kernel, [shaped((depth, rows, own * LANES)), window],
        [SMEM, SMEM] + [VMEM] * 7, scratch=scratch, input_output_aliases={5: 1},
    )(meta, z_taps, current, cur_b, obs, ratio, *mats)
    far = lax.ppermute(half, "view", swap)
    partial = call(
        place_kernel, shaped(estimate.shape), [SMEM, VMEM], HBM,
        scratch=[pltpu.SemaphoreType.DMA((depth,))],
    )(meta, half)
    return lax.dynamic_update_slice(partial, far, (0, 0, (1 - view) * own * LANES))


def extended_2(cells, sides, width):
    for axis, dim in sides:
        count = lax.axis_size(axis)
        ends = count - 1
        head = lax.slice_in_dim(cells, 0, width, axis=dim)
        tail = lax.slice_in_dim(cells, cells.shape[dim] - width, cells.shape[dim], axis=dim)
        cells = jnp.concatenate(
            [
                lax.ppermute(tail, axis, [(i, (i + 1) % count) for i in range(ends)]),
                cells,
                lax.ppermute(head, axis, [((i + 1) % count, i) for i in range(ends)]),
            ],
            axis=dim,
        )
    return cells


def band_matrix(taps, count_in, count_out, offset):
    rows_in = jnp.arange(count_in)[:, None]
    cols_out = jnp.arange(count_out)[None, :]
    lag = rows_in - cols_out + offset
    length = taps.shape[0]
    inside = (lag >= 0) & (lag < length)
    return jnp.where(inside, jnp.take(taps, jnp.clip(lag, 0, length - 1)), 0.0)


def many_bands(taps, count_in, count_out, offset):
    return jax.vmap(lambda one: band_matrix(one, count_in, count_out, offset))(taps)


def blur(field, z_mats, y_mats, x_taps, cols_out):
    highest = lax.Precision.HIGHEST
    if field.ndim == 3:
        out = jnp.einsum("kyx,vkz->vzyx", field, z_mats, precision=highest)
    else:
        out = jnp.einsum("vkyx,vkz->vzyx", field, z_mats, precision=highest)
    out = jnp.einsum("vzjx,vjy->vzyx", out, y_mats, precision=highest)
    reach = (x_taps.shape[1] - 1) // 2
    pieces = []
    for start in range(0, cols_out, 128):
        block = min(128, cols_out - start)
        x_mats = many_bands(x_taps, block + 2 * reach, block, 0)
        piece = lax.slice_in_dim(out, start, start + block + 2 * reach, axis=3)
        pieces.append(jnp.einsum("vzyj,vjx->vzyx", piece, x_mats, precision=highest))
    return jnp.concatenate(pieces, axis=3)


def body(estimate, observed, psf_taps):
    depth, rows, width = estimate.shape
    half = (psf_taps.shape[2] - 1) // 2
    views = lax.axis_size("view")
    recorded = lax.all_to_all(observed, "view", split_axis=3, concat_axis=0, tiled=True)
    taps = lax.all_gather(psf_taps, "view", axis=0, tiled=True)
    cols = width // views
    col_start = lax.axis_index("view") * cols
    current = lax.dynamic_slice_in_dim(estimate, col_start, cols, 2)
    normed = taps / jnp.sum(taps, axis=2, keepdims=True)
    flipped = normed[:, :, ::-1]
    fwd_z = many_bands(normed[:, 0], depth, depth, half)
    back_z = many_bands(flipped[:, 0], depth, depth, half)
    back_y = many_bands(flipped[:, 1], rows + 2 * half, rows, 0)
    fwd_y = many_bands(normed[:, 1], rows + 2 * half, rows, 0)
    for _ in range(ITERS):
        extended = extended_2(current, (("view", 2), ("tile", 1)), half)
        blurred = blur(extended, fwd_z, fwd_y, normed[:, 2], cols)
        ratio = recorded / blurred
        ratio_ext = extended_2(ratio, (("view", 3), ("tile", 2)), half)
        log_corr = jnp.log(blur(ratio_ext, back_z, back_y, flipped[:, 2], cols))
        log_total = jnp.sum(log_corr, axis=0)
        current = current * jnp.exp(log_total / views)
    current = lax.all_gather(current, "view", axis=2, tiled=True)
    return current


def fits(mesh, estimate, psf_taps):
    depth, rows, width = estimate.shape
    tiles = mesh.shape["tile"]
    reach = (psf_taps.shape[2] - 1) // 2
    return (
        mesh.shape["view"] == 2
        and tiles % 2 == 0
        and rows % (32 * tiles) == 0
        and rows // tiles >= 2 * (reach + 1)
        and width % (2 * LANES) == 0
        and 4 * reach <= LANES // 2
        and 2 * reach <= LANES // 4
        and depth % 4 == 0
    )


def solution(mesh):
    placed = (P(None, "tile", None), P("view", None, "tile", None), P("view", None, None))


    def run(estimate, observed, psf_taps):
        quick = fits(mesh, estimate, psf_taps)

        def chosen(*blocks):
            if not quick:
                return body(*blocks)
            return two_view_body(*blocks)

        step = jax.shard_map(
            chosen, mesh=mesh, in_specs=placed, out_specs=P(None, "tile", None), check_vma=False
        )
        return step(estimate, observed, psf_taps)

    return run
```

time: 48.2 us -> 51.4 us (1.066)
  the two profiles are of different devices: /device:TPU:18 before, /device:TPU:9 now
where the time goes in v3:
time: 51.4 us; the launch traced here: 51.2 us
  starting transfers between devices  20.3 us (39%)
  Pallas kernels  15.7 us (31%)
  waiting for transfers between devices  14 us (27%)
  local copies, waits for them, and re-layouts  0.72 us (1%)
    ppermute x4, starting transfers between devices, paired(): got_b = lax.ppermute(cells_b, 'tile', pairs_b)  16 us
    ppermute x4, waiting for transfers between devices, paired(): got_b = lax.ppermute(cells_b, 'tile', pairs_b)  7.84 us
    ppermute x1, waiting for transfers between devices, two_view_body(): far = lax.ppermute(half, 'view', swap)  5.28 us
    pallas_call x1, Pallas kernels, two_view_body(): call(second_b_kernel, [shaped((depth, rows, own * LANES)), window], [SMEM...  3.33 us
    pallas_call x1, Pallas kernels, two_view_body(): call(first_kernel, [window, window], [SMEM, SMEM] + [VMEM] * 9, scratch=[...  2.81 us
    pallas_call x1, Pallas kernels, two_view_body(): call(load_kernel, [shaped(cells.shape) for cells in (estimate, observed,...  2.39 us
    pallas_call x1, Pallas kernels, two_view_body(): call(update_kernel, [window, window, shaped((depth, rows, lanes)), shaped...  2.32 us
    pallas_call x1, Pallas kernels, two_view_body(): call(second_a_kernel, window, [SMEM, SMEM] + [VMEM] * 6, scratch=scratch)  1.89 us
  transfers between devices with their start and end apart: 12, of which 4 were waited for; matrix products, arithmetic and copies ran while one was open for 0% of the time, Pallas kernels for 15%

profile of v3, /device:TPU:9, one launch (start us, length us, event | category | flops | bytes accessed | tf_op | source)
XLA Modules:
  0.0 51.2 jit_solution(13060743548399792277)
XLA Ops:
  0.0 0.1 pad_add_fusion.meta
  0.1 2.4 %shard_map.37 = (f32[8,32,512]{2,1,0:T(8,128)S(1)}, f32[1,8,32,512]{3,2,1,0:T(8,128)S(1)}, f32[3,1,31]{2,1,0:T(1,128)S(1)}, f32[20,32,128]{2,1,0:T(8,128)S(1)}, ...) custom-call(s32[4]{0:T(128)S(1)} %pad_add_fusion.meta, ...), custom_call_target="tpu_custom_call" | custom-call | tf_op jit(solution)/shard_map/pallas_call | solution.py:464
  2.5 3.7 %collective-permute-start.2 = (f32[20,32,128]{2,1,0:T(8,128)S(1)}, f32[20,32,128]{2,1,0:T(8,128)S(1)}, u32[]{:S(2)}, u32[]{:S(2)}) collective-permute-start(f32[20,32,128]{2,1,0:T(8,128)S(1)} %get-tuple-element.25), channel_id=1, source_target_pairs={{1,2},{2,1},{3,4},{4,3},{5,6},{6,5},{7,8},{8,7},{9,10},{10,9},{11,... | collective-permute-start | bytes 983048 | tf_op jit(solution)/shard_map/ppermute | solution.py:441
  6.2 1.3 %collective-permute-start = (f32[3,1,31]{2,1,0:T(1,128)S(1)}, f32[3,1,31]{2,1,0:T(1,128)S(1)}, u32[]{:S(2)}, u32[]{:S(2)}) collective-permute-start(f32[3,1,31]{2,1,0:T(1,128)S(1)} %get-tuple-element.22), channel_id=1, source_target_pairs={{0,16},{16,0},{1,17},{17,1},{2,18},{18,2},{3,19},{19,3},{4,20},{20... | collective-permute-start | bytes 1124 | tf_op jit(solution)/shard_map/ppermute | solution.py:474
  7.5 0.2 collective-permute-start.3
  7.7 1.2 %collective-permute-start.4 = (f32[20,16,128]{2,1,0:T(8,128)S(1)}, f32[20,16,128]{2,1,0:T(8,128)S(1)}, u32[]{:S(2)}, u32[]{:S(2)}) collective-permute-start(f32[20,16,128]{2,1,0:T(8,128)S(1)} %get-tuple-element.27), channel_id=1, source_target_pairs={{0,16},{16,0},{1,17},{17,1},{2,18},{18,2},{3,19},{19,3},{4,20},{20... | collective-permute-start | bytes 491528 | tf_op jit(solution)/shard_map/ppermute | solution.py:472
  9.0 1.1 %collective-permute-start.5 = (f32[20,16,128]{2,1,0:T(8,128)S(1)}, f32[20,16,128]{2,1,0:T(8,128)S(1)}, u32[]{:S(2)}, u32[]{:S(2)}) collective-permute-start(f32[20,16,128]{2,1,0:T(8,128)S(1)} %get-tuple-element.33), channel_id=1, source_target_pairs={{0,1},{1,0},{2,3},{3,2},{4,5},{5,4},{6,7},{7,6},{8,9},{9,8},{10,11... | collective-permute-start | bytes 491528 | tf_op jit(solution)/shard_map/ppermute | solution.py:442
  10.0 0.1 fusion
  10.1 0.1 broadcast_divide_fusion.taps
  10.2 1.6 %shard_map.38 = (bf16[2,2,32,192]{3,2,1,0:T(8,128)(2,1)S(1)}, bf16[2,2,1152,256]{3,2,1,0:T(8,128)(2,1)S(1)}, bf16[2,2,768,128]{3,2,1,0:T(8,128)(2,1)S(1)}) custom-call(s32[4]{0:T(128)S(1)} %pad_add_fusion.meta, f32[3,2,31]{2,1,0:T(2,128)S(1)} %broadcast_divide_fusion.taps), custom_call_target="tpu_custom_call" | custom-call | tf_op jit(solution)/shard_map/pallas_call | solution.py:480
  11.8 0.9 %collective-permute-done.3.other_a = f32[20,16,128]{2,1,0:T(8,128)S(1)} collective-permute-done((f32[20,16,128]{2,1,0:T(8,128)S(1)}, f32[20,16,128]{2,1,0:T(8,128)S(1)}, u32[]{:S(2)}, u32[]{:S(2)}) %collective-permute-start.3) | collective-permute-done | bytes 163872 | tf_op jit(solution)/shard_map/ppermute | solution.py:473
  12.7 5.4 %collective-permute-start.6 = (f32[20,16,128]{2,1,0:T(8,128)S(1)}, f32[20,16,128]{2,1,0:T(8,128)S(1)}, u32[]{:S(2)}, u32[]{:S(2)}) collective-permute-start(f32[20,16,128]{2,1,0:T(8,128)S(1)} %get-tuple-element.34), channel_id=1, source_target_pairs={{1,2},{2,1},{3,4},{4,3},{5,6},{6,5},{7,8},{8,7},{9,10},{10,9},{11,... | collective-permute-start | bytes 491528 | tf_op jit(solution)/shard_map/ppermute | solution.py:441
  18.2 3.5 %collective-permute-start.8 = (f32[20,16,128]{2,1,0:T(8,128)S(1)}, f32[20,16,128]{2,1,0:T(8,128)S(1)}, u32[]{:S(2)}, u32[]{:S(2)}) collective-permute-start(f32[20,16,128]{2,1,0:T(8,128)S(1)} %collective-permute-done.4.other_b), channel_id=1, source_target_pairs={{1,2},{2,1},{3,4},{4,3},{5,6},{6,5},{7,8},{8,7},{9,10},{10,9},{11,... | collective-permute-start | bytes 491528 | tf_op jit(solution)/shard_map/ppermute | solution.py:441
  21.7 2.8 %shard_map.39 = (f32[2,8,64,384]{3,2,1,0:T(8,128)S(1)}, f32[2,8,64,384]{3,2,1,0:T(8,128)S(1)}) custom-call(s32[4]{0:T(128)S(1)} %pad_add_fusion.meta, f32[2,31]{1,0:T(2,128)S(1)} %slice_bitcast_fusion.z_taps, f32[8,32,512]{2,1,0:T(8,128)S(1)} %get-tuple-element.23.est, f32[1,8,32,512]{3,2,1,0:T(8,128)S(1)} %get-tuple-element.24.obs_own, ...), custom_call_target="tpu_custom_call" | custom-call | tf_op jit(solution)/shard_map/pallas_call | solution.py:495
  24.6 2.0 %collective-permute-done.8.far_b = f32[20,16,128]{2,1,0:T(8,128)S(1)} collective-permute-done((f32[20,16,128]{2,1,0:T(8,128)S(1)}, f32[20,16,128]{2,1,0:T(8,128)S(1)}, u32[]{:S(2)}, u32[]{:S(2)}) %collective-permute-start.8) | collective-permute-done | bytes 163872 | tf_op jit(solution)/shard_map/ppermute | solution.py:441
  26.6 2.3 %shard_map.40 = (f32[2,8,64,384]{3,2,1,0:T(8,128)S(1)}, f32[2,8,64,384]{3,2,1,0:T(8,128)S(1)}, f32[8,32,384]{2,1,0:T(8,128)S(1)}, f32[18,32,128]{2,1,0:T(8,128)S(1)}) custom-call(s32[4]{0:T(128)S(1)} %pad_add_fusion.meta, f32[2,31]{1,0:T(2,128)S(1)} %slice_bitcast_fusion.z_taps, ...), custom_call_target="tpu_custom_call", output_to_operand_aliasing={{0}: (3, {}), {1}: (4, {})} | custom-call | tf_op jit(solution)/shard_map/pallas_call | solution.py:502
  29.0 3.5 %collective-permute-start.9 = (f32[18,32,128]{2,1,0:T(8,128)S(1)}, f32[18,32,128]{2,1,0:T(8,128)S(1)}, u32[]{:S(2)}, u32[]{:S(2)}) collective-permute-start(f32[18,32,128]{2,1,0:T(8,128)S(1)} %get-tuple-element.36), channel_id=1, source_target_pairs={{1,2},{2,1},{3,4},{4,3},{5,6},{6,5},{7,8},{8,7},{9,10},{10,9},{11,... | collective-permute-start | bytes 884744 | tf_op jit(solution)/shard_map/ppermute | solution.py:441
  32.5 1.9 %shard_map.41.ratio_in = f32[2,8,64,384]{3,2,1,0:T(8,128)S(1)} custom-call(s32[4]{0:T(128)S(1)} %pad_add_fusion.meta, f32[2,31]{1,0:T(2,128)S(1)} %slice_bitcast_fusion.z_taps, f32[8,32,384]{2,1,0:T(8,128)S(1)} %get-tuple-element.35.current, f32[18,32,128]{2,1,0:T(8,128)S(1)} %collective-permute-done.10.got_a, f32[2,8,64,384]{3,2,1,0:T(8,128)S(1)} %get-tuple-element.37.obs, ...), custom_call_target="tpu_custom_call" | custom-call | tf_op jit(solution)/shard_map/pallas_call | solution.py:508
  34.4 5.8 %collective-permute-done.9.got_b = f32[18,32,128]{2,1,0:T(8,128)S(1)} collective-permute-done((f32[18,32,128]{2,1,0:T(8,128)S(1)}, f32[18,32,128]{2,1,0:T(8,128)S(1)}, u32[]{:S(2)}, u32[]{:S(2)}) %collective-permute-start.9) | collective-permute-done | bytes 294944 | tf_op jit(solution)/shard_map/ppermute | solution.py:441
  40.2 3.3 %shard_map.42 = (f32[8,32,256]{2,1,0:T(8,128)S(1)}, f32[2,8,64,384]{3,2,1,0:T(8,128)S(1)}) custom-call(s32[4]{0:T(128)S(1)} %pad_add_fusion.meta, f32[2,31]{1,0:T(2,128)S(1)} %slice_bitcast_fusion.z_taps, f32[8,32,384]{2,1,0:T(8,128)S(1)} %get-tuple-element.35.current, ...), custom_call_target="tpu_custom_call", output_to_operand_aliasing={{1}: (5, {})} | custom-call | tf_op jit(solution)/shard_map/pallas_call | solution.py:511
  43.6 0.3 collective-permute-start.11
  43.9 1.3 %shard_map.43 = f32[8,32,512]{2,1,0:T(8,128)} custom-call(s32[4]{0:T(128)S(1)} %pad_add_fusion.meta, f32[8,32,256]{2,1,0:T(8,128)S(1)} %get-tuple-element.38.half), custom_call_target="tpu_custom_call" | custom-call | tf_op jit(solution)/shard_map/pallas_call | solution.py:516
  45.2 5.3 %collective-permute-done.11 = f32[8,32,256]{2,1,0:T(8,128)S(1)} collective-permute-done((f32[8,32,256]{2,1,0:T(8,128)S(1)}, f32[8,32,256]{2,1,0:T(8,128)S(1)}, u32[]{:S(2)}, u32[]{:S(2)}) %collective-permute-start.11) | collective-permute-done | bytes 262176 | tf_op jit(solution)/shard_map/ppermute | solution.py:515
  50.4 0.7 %constant_dynamic-update-slice_fusion = f32[8,32,512]{2,1,0:T(8,128)} fusion(f32[8,32,512]{2,1,0:T(8,128)} %shard_map.43, f32[8,32,256]{2,1,0:T(8,128)S(1)} %collective-permute-done.11, s32[]{:T(128)S(6)} %select_n.3), kind=kLoop, calls=%fused_computation.5 | loop fusion | bytes 524292 | tf_op jit(solution)/shard_map/dynamic_update_slice | solution.py:520
  (12 shorter events, 0.2 us)
Async XLA Ops:
  2.5 15.7 %collective-permute-start.2 = (f32[20,32,128]{2,1,0:T(8,128)S(1)}, f32[20,32,128]{2,1,0:T(8,128)S(1)}, u32[]{:S(2)}, u32[]{:S(2)}) collective-permute-start(f32[20,32,128]{2,1,0:T(8,128)S(1)} %get-tuple-element.25), channel_id=1, source_target_pairs={{1,2},{2,1},{3,4},{4,3},{5,6},{6,5},{7,8},{8,7},{9,10},{10,9},{11,... | collective-permute-start | bytes 983048 | tf_op jit(solution)/shard_map/ppermute | solution.py:441
  6.2 2.8 %collective-permute-start = (f32[3,1,31]{2,1,0:T(1,128)S(1)}, f32[3,1,31]{2,1,0:T(1,128)S(1)}, u32[]{:S(2)}, u32[]{:S(2)}) collective-permute-start(f32[3,1,31]{2,1,0:T(1,128)S(1)} %get-tuple-element.22), channel_id=1, source_target_pairs={{0,16},{16,0},{1,17},{17,1},{2,18},{18,2},{3,19},{19,3},{4,20},{20... | collective-permute-start | bytes 1124 | tf_op jit(solution)/shard_map/ppermute | solution.py:474
  7.5 14.2 %collective-permute-start.1 = (f32[20,32,128]{2,1,0:T(8,128)S(1)}, f32[20,32,128]{2,1,0:T(8,128)S(1)}, u32[]{:S(2)}, u32[]{:S(2)}) collective-permute-start(f32[20,32,128]{2,1,0:T(8,128)S(1)} %get-tuple-element.25), channel_id=1, source_target_pairs={{0,1},{1,0},{2,3},{3,2},{4,5},{5,4},{6,7},{7,6},{8,9},{9,8},{10,11... | collective-permute-start | bytes 983048 | tf_op jit(solution)/shard_map/ppermute | solution.py:442
  7.5 5.2 %collective-permute-start.3 = (f32[20,16,128]{2,1,0:T(8,128)S(1)}, f32[20,16,128]{2,1,0:T(8,128)S(1)}, u32[]{:S(2)}, u32[]{:S(2)}) collective-permute-start(f32[20,16,128]{2,1,0:T(8,128)S(1)} %get-tuple-element.26), channel_id=1, source_target_pairs={{0,16},{16,0},{1,17},{17,1},{2,18},{18,2},{3,19},{19,3},{4,20},{20... | collective-permute-start | bytes 491528 | tf_op jit(solution)/shard_map/ppermute | solution.py:473
  7.7 10.4 %collective-permute-start.4 = (f32[20,16,128]{2,1,0:T(8,128)S(1)}, f32[20,16,128]{2,1,0:T(8,128)S(1)}, u32[]{:S(2)}, u32[]{:S(2)}) collective-permute-start(f32[20,16,128]{2,1,0:T(8,128)S(1)} %get-tuple-element.27), channel_id=1, source_target_pairs={{0,16},{16,0},{1,17},{17,1},{2,18},{18,2},{3,19},{19,3},{4,20},{20... | collective-permute-start | bytes 491528 | tf_op jit(solution)/shard_map/ppermute | solution.py:472
  9.0 15.6 %collective-permute-start.5 = (f32[20,16,128]{2,1,0:T(8,128)S(1)}, f32[20,16,128]{2,1,0:T(8,128)S(1)}, u32[]{:S(2)}, u32[]{:S(2)}) collective-permute-start(f32[20,16,128]{2,1,0:T(8,128)S(1)} %get-tuple-element.33), channel_id=1, source_target_pairs={{0,1},{1,0},{2,3},{3,2},{4,5},{5,4},{6,7},{7,6},{8,9},{9,8},{10,11... | collective-permute-start | bytes 491528 | tf_op jit(solution)/shard_map/ppermute | solution.py:442
  12.7 11.8 %collective-permute-start.6 = (f32[20,16,128]{2,1,0:T(8,128)S(1)}, f32[20,16,128]{2,1,0:T(8,128)S(1)}, u32[]{:S(2)}, u32[]{:S(2)}) collective-permute-start(f32[20,16,128]{2,1,0:T(8,128)S(1)} %get-tuple-element.34), channel_id=1, source_target_pairs={{1,2},{2,1},{3,4},{4,3},{5,6},{6,5},{7,8},{8,7},{9,10},{10,9},{11,... | collective-permute-start | bytes 491528 | tf_op jit(solution)/shard_map/ppermute | solution.py:441
  18.1 6.4 %collective-permute-start.7 = (f32[20,16,128]{2,1,0:T(8,128)S(1)}, f32[20,16,128]{2,1,0:T(8,128)S(1)}, u32[]{:S(2)}, u32[]{:S(2)}) collective-permute-start(f32[20,16,128]{2,1,0:T(8,128)S(1)} %collective-permute-done.3.other_a), channel_id=1, source_target_pairs={{0,1},{1,0},{2,3},{3,2},{4,5},{5,4},{6,7},{7,6},{8,9},{9,8},{10,11... | collective-permute-start | bytes 491528 | tf_op jit(solution)/shard_map/ppermute | solution.py:442
  18.2 8.4 %collective-permute-start.8 = (f32[20,16,128]{2,1,0:T(8,128)S(1)}, f32[20,16,128]{2,1,0:T(8,128)S(1)}, u32[]{:S(2)}, u32[]{:S(2)}) collective-permute-start(f32[20,16,128]{2,1,0:T(8,128)S(1)} %collective-permute-done.4.other_b), channel_id=1, source_target_pairs={{1,2},{2,1},{3,4},{4,3},{5,6},{6,5},{7,8},{8,7},{9,10},{10,9},{11,... | collective-permute-start | bytes 491528 | tf_op jit(solution)/shard_map/ppermute | solution.py:441
  28.9 3.6 %collective-permute-start.10 = (f32[18,32,128]{2,1,0:T(8,128)S(1)}, f32[18,32,128]{2,1,0:T(8,128)S(1)}, u32[]{:S(2)}, u32[]{:S(2)}) collective-permute-start(f32[18,32,128]{2,1,0:T(8,128)S(1)} %get-tuple-element.36), channel_id=1, source_target_pairs={{0,1},{1,0},{2,3},{3,2},{4,5},{5,4},{6,7},{7,6},{8,9},{9,8},{10,11... | collective-permute-start | bytes 884744 | tf_op jit(solution)/shard_map/ppermute | solution.py:442
  29.0 11.2 %collective-permute-start.9 = (f32[18,32,128]{2,1,0:T(8,128)S(1)}, f32[18,32,128]{2,1,0:T(8,128)S(1)}, u32[]{:S(2)}, u32[]{:S(2)}) collective-permute-start(f32[18,32,128]{2,1,0:T(8,128)S(1)} %get-tuple-element.36), channel_id=1, source_target_pairs={{1,2},{2,1},{3,4},{4,3},{5,6},{6,5},{7,8},{8,7},{9,10},{10,9},{11,... | collective-permute-start | bytes 884744 | tf_op jit(solution)/shard_map/ppermute | solution.py:441
  43.6 6.9 %collective-permute-start.11 = (f32[8,32,256]{2,1,0:T(8,128)S(1)}, f32[8,32,256]{2,1,0:T(8,128)S(1)}, u32[]{:S(2)}, u32[]{:S(2)}) collective-permute-start(f32[8,32,256]{2,1,0:T(8,128)S(1)} %get-tuple-element.38.half), channel_id=1, source_target_pairs={{0,16},{16,0},{1,17},{17,1},{2,18},{18,2},{3,19},{19,3},{4,20},{20... | collective-permute-start | bytes 786440 | tf_op jit(solution)/shard_map/ppermute | solution.py:515
